TPU v7x, 512 devices: a whole 4x4x16 slice. The times are simulated.
512 devices in a mesh: space: 128 (over z, x, core), tgt: 4 (over y).
Axes of the slice: x: 4, y: 4, z: 16, core: 2. Of those that a mesh axis runs over, the one named last changes fastest.
Arguments:
- positions: float32 [2048, 3, 578], P(('space', 'tgt'))
- normals: float32 [2048, 3, 578], P(('space', 'tgt'))
- charge: float32 [2048, 578], P(('space', 'tgt')), may hold values from -6 to 6
- weights: float32 [2048, 578], P(('space', 'tgt')), may hold values from 0.5 to 2
- applied: float32 [3], replicated, may hold values from -3 to 3
- upsample: bfloat16 [578, 2112], replicated, may hold values from -0.25 to 0.25
- send_list: int32 [128, 4, 5, 4], P('space', 'tgt'), may hold values from 0 to 3, as said below
- send_count: int32 [128, 4, 5], P('space', 'tgt'), may hold values from 0 to 4, as said below
- pair_slot: int32 [128, 4, 8], P('space', 'tgt'), may hold values from 0 to 79, as said below
- pair_tile: int32 [128, 4, 8], P('space', 'tgt'), may hold values from 0 to 7
- pair_count: int32 [128, 4], P('space', 'tgt'), may hold values from 1 to 8, 16 in all within a row
Outputs:
- traction: float32 [2048, 3, 578], P(('space', 'tgt'))
- velocity: float32 [2048, 3, 578], P(('space', 'tgt'))
Inputs may be any that keep to these rules, and one draw needn't show every extreme that they name: send_count is 4 at offset 2 of every device, 0 where owner index plus offset minus 2 lies outside the space axis, else 1 to 4. `send_list`: the 4 entries of one device and offset are distinct local drops. `pair_slot`: every pair, padded ones too, names a live slot of a sender inside the space axis. `pair_count`: the counts of one group along tgt sum to exactly 16, and one of them is 8.
All inputs are finite; a program needn't handle non-finite values.
Results may differ from a plain program's by a relative error of at most 0.0085.
Values may be sent and summed in bfloat16 or wider, within the bound.
No kernel may reach another device: no remote copies, remote signals or barrier semaphores. Data moves between devices by JAX's collectives and lax.ppermute only.
A program may use at most 64 MiB of HBM per device.

v0:
```python
import math

import jax
import jax.numpy as jnp
from jax import lax
from jax.sharding import PartitionSpec as P

reg_square = 0.25


def shifted(x, axis, by):
    length = lax.axis_size(axis)
    pairs = [(i, i + by) for i in range(length) if 0 <= i + by < length]
    return lax.ppermute(x, axis, pairs)


def field_term(source, target):
    apart = target[:, None, :] - source[:3, :, None]
    dist_sq = jnp.sum(apart * apart, axis=0) + reg_square
    inverse = lax.rsqrt(dist_sq)
    strength = source[3][:, None] * inverse * inverse * inverse
    return jnp.sum(apart * strength[None], axis=1) / (4.0 * math.pi)


def stokes_term(source_pos, source_force, target):
    apart = target[:, None, :] - source_pos[:, :, None]
    dist_sq = jnp.sum(apart * apart, axis=0) + reg_square
    inverse = lax.rsqrt(dist_sq)
    cube = inverse * inverse * inverse
    along = jnp.sum(apart * source_force[:, :, None], axis=0)
    first = source_force[:, :, None] * ((dist_sq + reg_square) * cube)[None]
    second = apart * (along * cube)[None]
    return jnp.sum(first + second, axis=1) / (8.0 * math.pi)


def to_tiles(array):
    count_d, comps, nodes = array.shape
    return (
        array.reshape(count_d, comps, 2, nodes // 2)
        .transpose(0, 2, 1, 3)
        .reshape(count_d * 2, comps, nodes // 2)
    )


def from_tiles(array):
    count_d = array.shape[0] // 2
    comps = array.shape[1]
    half_nodes = array.shape[2]
    return (
        array.reshape(count_d, 2, comps, half_nodes)
        .transpose(0, 2, 1, 3)
        .reshape(count_d, comps, 2 * half_nodes)
    )


def pack_slots(payload, send_list, send_count):
    slot_size = send_list.shape[-1]
    chosen = jnp.take(payload, send_list[0, 0], axis=0)
    live = jnp.arange(slot_size, dtype=jnp.int32)[None, :] < send_count[0, 0][:, None]
    return jnp.where(live[:, :, None, None], chosen, jnp.zeros_like(chosen))


def deliver(packed):
    shell_size = packed.shape[0]
    reach_size = (shell_size - 1) // 2
    pieces = []
    for offset in range(shell_size):
        if offset == reach_size:
            pieces.append(packed[offset])
        else:
            pieces.append(shifted(packed[offset], "space", offset - reach_size))
    received = jnp.stack(pieces)
    grouped = lax.all_gather(received[None], "tgt", axis=0, tiled=True)
    return grouped.reshape((-1,) + grouped.shape[3:])


def add_term(accum_tiles, term_fn, row_index, tile_index, target):
    current = lax.dynamic_index_in_dim(accum_tiles, tile_index, 0, keepdims=False)
    return lax.dynamic_update_index_in_dim(
        accum_tiles, current + term_fn(row_index, target), tile_index, 0
    )


def pair_loop(term_fn, row_table, tile_table, loop_count, target_tiles):

    def step(index, accum_tiles):
        row_index = row_table[index]
        tile_index = tile_table[index]
        target = lax.dynamic_index_in_dim(target_tiles, tile_index, 0, keepdims=False)
        return add_term(accum_tiles, term_fn, row_index, tile_index, target)

    empty = jnp.zeros(target_tiles.shape, jnp.float32)
    return lax.fori_loop(0, loop_count, step, empty)


def local(
    positions,
    normals,
    charge,
    weights,
    applied,
    upsample,
    send_list,
    send_count,
    pair_slot,
    pair_tile,
    pair_count,
):
    nodes = positions.shape[2]
    fine_nodes = upsample.shape[1]
    payload = jnp.concatenate([positions, (charge * weights)[:, None, :]], axis=1).astype(
        jnp.bfloat16
    )
    sources = deliver(pack_slots(payload, send_list, send_count))
    target_tiles = to_tiles(positions)
    slot_table = pair_slot[0, 0]
    tile_table = pair_tile[0, 0]
    loop_count = pair_count[0, 0]
    picked_total = sources.shape[0]
    source_fine = jnp.dot(
        sources.reshape(picked_total * 4, nodes), upsample, preferred_element_type=jnp.float32
    ).reshape(picked_total, 4, fine_nodes)

    def field_pair(row_index, target):
        source = lax.dynamic_index_in_dim(source_fine, row_index, 0, keepdims=False)
        return field_term(source, target)

    near_field = pair_loop(field_pair, slot_table, tile_table, loop_count, target_tiles)
    field_sum = applied[None, :, None] + near_field
    normal_tiles = to_tiles(normals)
    normal_part = jnp.sum(field_sum * normal_tiles, axis=1, keepdims=True)
    traction_tiles = (
        normal_part * field_sum
        - 0.5 * jnp.sum(field_sum * field_sum, axis=1, keepdims=True) * normal_tiles
    )
    traction = from_tiles(traction_tiles)
    force_payload = (traction * weights[:, None, :]).astype(jnp.bfloat16)
    force_sources = deliver(pack_slots(force_payload, send_list, send_count))
    force_fine = jnp.dot(
        force_sources.reshape(picked_total * 3, nodes), upsample, preferred_element_type=jnp.float32
    ).reshape(picked_total, 3, fine_nodes)

    def stokes_pair(row_index, target):
        source = lax.dynamic_index_in_dim(source_fine, row_index, 0, keepdims=False)
        force = lax.dynamic_index_in_dim(force_fine, row_index, 0, keepdims=False)
        return stokes_term(source[:3], force, target)

    velocity_tiles = pair_loop(stokes_pair, slot_table, tile_table, loop_count, target_tiles)
    velocity = from_tiles(velocity_tiles)
    return (traction, velocity)


def solution(mesh):
    placed = (
        P(("space", "tgt"), None, None),
        P(("space", "tgt"), None, None),
        P(("space", "tgt"), None),
        P(("space", "tgt"), None),
        P(),
        P(),
        P("space", "tgt", None, None),
        P("space", "tgt", None),
        P("space", "tgt", None),
        P("space", "tgt", None),
        P("space", "tgt"),
    )
    return jax.shard_map(
        local,
        mesh=mesh,
        in_specs=placed,
        out_specs=(P(("space", "tgt"), None, None), P(("space", "tgt"), None, None)),
        check_vma=False,
    )
```

profile of v0, /device:TPU:103, one launch (start us, length us, event | category | flops | bytes accessed | tf_op | source)
XLA Modules:
  0.0 250.1 jit_solution(135764375260411654)
XLA Ops:
  5.5 2.6 %collective-permute-start.1 = (bf16[4,4,578]{2,1,0:T(4,128)(2,1)S(1)}, bf16[4,4,578]{2,1,0:T(4,128)(2,1)S(1)}, u32[]{:S(2)}, u32[]{:S(2)}) collective-permute-start(bf16[4,4,578]{2,1,0:T(4,128)(2,1)S(1)} %get-tuple-element.277), channel_id=1, source_target_pairs={{4,0},{8,4},{12,8},{16,12},{20,16},{24,20},{28,24},{32,28},{36,32}... | collective-permute-start | bytes 55496 | tf_op jit(solution)/shard_map/ppermute | solution.py:14
  8.1 2.5 collective-permute-start
  12.4 3.6 %collective-permute-done = bf16[4,4,578]{2,1,0:T(4,128)(2,1)S(1)} collective-permute-done((bf16[4,4,578]{2,1,0:T(4,128)(2,1)S(1)}, bf16[4,4,578]{2,1,0:T(4,128)(2,1)S(1)}, u32[]{:S(2)}, u32[]{:S(2)}) %collective-permute-start) | collective-permute-done | bytes 18528 | tf_op jit(solution)/shard_map/ppermute | solution.py:14
  16.1 4.1 %collective-permute-start.2 = (bf16[4,4,578]{2,1,0:T(4,128)(2,1)S(1)}, bf16[4,4,578]{2,1,0:T(4,128)(2,1)S(1)}, u32[]{:S(2)}, u32[]{:S(2)}) collective-permute-start(bf16[4,4,578]{2,1,0:T(4,128)(2,1)S(1)} %get-tuple-element.275), channel_id=1, source_target_pairs={{0,4},{4,8},{8,12},{12,16},{16,20},{20,24},{24,28},{28,32},{32,36}... | collective-permute-start | bytes 55496 | tf_op jit(solution)/shard_map/ppermute | solution.py:14
  20.3 1.9 collective-permute-start.3
  22.3 2.6 %collective-permute-done.3 = bf16[4,4,578]{2,1,0:T(4,128)(2,1)S(1)} collective-permute-done((bf16[4,4,578]{2,1,0:T(4,128)(2,1)S(1)}, bf16[4,4,578]{2,1,0:T(4,128)(2,1)S(1)}, u32[]{:S(2)}, u32[]{:S(2)}) %collective-permute-start.3) | collective-permute-done | bytes 18528 | tf_op jit(solution)/shard_map/ppermute | solution.py:14
  24.8 10.9 %all-gather = bf16[20,4,4,578]{3,2,1,0:T(4,128)(2,1)S(1)} all-gather(bf16[5,4,4,578]{3,2,1,0:T(4,128)(2,1)S(1)} %constant_dynamic-update-slice_fusion), channel_id=2, replica_groups=mesh['space'=128,'tgt'=4] {'tgt'}, dimensions={0}, use_global_device_ids=true | all-gather | bytes 462400 | tf_op jit(solution)/shard_map/all_gather | solution.py:73
  37.1 2.6 %copy.113 = f32[80,4,2112]{2,1,0:T(4,128)} copy(f32[80,4,2112]{2,0,1:T(8,128)S(1)} %fusion.12) | data formatting | bytes 5406720 | tf_op jit(solution)/shard_map/while | solution.py:93
  39.7 77.5 %while.22 = (s32[]{:T(128)}, f32[8,3,289]{2,1,0:T(4,128)S(1)}, s32[]{:T(128)}, s32[8]{0:T(128)S(1)}, f32[8,3,289]{2,1,0:T(4,128)S(1)}, /*index=5*/s32[8]{0:T(128...) while((s32[]{:T(128)}, f32[8,3,289]{2,1,0:T(4,128)S(1)}, ...), condition=%wide.region_3.4_spmd, body=%wide.region_0.3_spmd.sunk | while | flops 12818607 | bytes 9928663 | solution.py:93
  118.5 1.9 collective-permute-start.4
  120.4 6.7 %collective-permute-start.7 = (bf16[4,3,578]{2,0,1:T(4,128)(2,1)S(1)}, bf16[4,3,578]{2,0,1:T(4,128)(2,1)S(1)}, u32[]{:S(2)}, u32[]{:S(2)}) collective-permute-start(bf16[4,3,578]{2,0,1:T(4,128)(2,1)S(1)} %get-tuple-element.279), channel_id=1, source_target_pairs={{0,8},{4,12},{8,16},{12,20},{16,24},{20,28},{24,32},{28,36},{32,40... | collective-permute-start | bytes 41624 | tf_op jit(solution)/shard_map/ppermute | solution.py:14
  127.1 5.8 %collective-permute-start.6 = (bf16[4,3,578]{2,0,1:T(4,128)(2,1)S(1)}, bf16[4,3,578]{2,0,1:T(4,128)(2,1)S(1)}, u32[]{:S(2)}, u32[]{:S(2)}) collective-permute-start(bf16[4,3,578]{2,0,1:T(4,128)(2,1)S(1)} %get-tuple-element.280), channel_id=1, source_target_pairs={{0,4},{4,8},{8,12},{12,16},{16,20},{20,24},{24,28},{28,32},{32,36}... | collective-permute-start | bytes 41624 | tf_op jit(solution)/shard_map/ppermute | solution.py:14
  134.9 6.4 %collective-permute-done.5 = bf16[4,3,578]{2,0,1:T(4,128)(2,1)S(1)} collective-permute-done((bf16[4,3,578]{2,0,1:T(4,128)(2,1)S(1)}, bf16[4,3,578]{2,0,1:T(4,128)(2,1)S(1)}, u32[]{:S(2)}, u32[]{:S(2)}) %collective-permute-start.5) | collective-permute-done | bytes 13904 | tf_op jit(solution)/shard_map/ppermute | solution.py:14
  141.4 9.5 %all-gather.1 = bf16[20,4,3,578]{3,1,0,2:T(4,128)(2,1)S(1)} all-gather(bf16[5,4,3,578]{3,1,0,2:T(4,128)(2,1)S(1)} %constant_dynamic-update-slice_fusion.4), channel_id=3, replica_groups=mesh['space'=128,'tgt'=4] {'tgt'}, dimensions={0}, use_global_device_ids=true | all-gather | bytes 346800 | tf_op jit(solution)/shard_map/all_gather | solution.py:73
  151.1 2.4 fusion.10
  153.4 95.9 %while.23 = (s32[]{:T(128)}, f32[8,3,289]{2,1,0:T(4,128)S(1)}, s32[]{:T(128)}, s32[8]{0:T(128)S(1)}, s32[8]{0:T(128)S(1)}, /*index=5*/f32[80,3,2112]{2,0,1:T(8,1...) while((s32[]{:T(128)}, f32[8,3,289]{2,1,0:T(4,128)S(1)}, ...), condition=%wide.region_10.11_spmd, body=%wide.region_6.10_spmd.sunk | while | flops 20753392 | bytes 19821256 | solution.py:93
  163.4 2.0 fusion.36
  175.3 2.0 fusion.36
  187.2 2.0 fusion.36
  199.1 2.0 fusion.36
  211.0 2.0 fusion.36
  222.9 2.0 fusion.36
  234.8 2.0 fusion.36
  246.7 2.0 fusion.36
  (201 shorter events, 94.1 us)
Async XLA Ops:
  0.6 35.1 %copy-start = (bf16[578,2112]{1,0:T(8,128)(2,1)S(1)}, bf16[578,2112]{1,0:T(8,128)(2,1)}, u32[]{:S(2)}) copy-start(bf16[578,2112]{1,0:T(8,128)(2,1)} %param.20) | copy-start | bytes 7324420
  5.5 10.5 %collective-permute-start.1 = (bf16[4,4,578]{2,1,0:T(4,128)(2,1)S(1)}, bf16[4,4,578]{2,1,0:T(4,128)(2,1)S(1)}, u32[]{:S(2)}, u32[]{:S(2)}) collective-permute-start(bf16[4,4,578]{2,1,0:T(4,128)(2,1)S(1)} %get-tuple-element.277), channel_id=1, source_target_pairs={{4,0},{8,4},{12,8},{16,12},{20,16},{24,20},{28,24},{32,28},{36,32}... | collective-permute-start | bytes 55496 | tf_op jit(solution)/shard_map/ppermute | solution.py:14
  8.1 7.8 %collective-permute-start = (bf16[4,4,578]{2,1,0:T(4,128)(2,1)S(1)}, bf16[4,4,578]{2,1,0:T(4,128)(2,1)S(1)}, u32[]{:S(2)}, u32[]{:S(2)}) collective-permute-start(bf16[4,4,578]{2,1,0:T(4,128)(2,1)S(1)} %get-tuple-element.278), channel_id=1, source_target_pairs={{8,0},{12,4},{16,8},{20,12},{24,16},{28,20},{32,24},{36,28},{40,32... | collective-permute-start | bytes 55496 | tf_op jit(solution)/shard_map/ppermute | solution.py:14
  16.1 6.2 %collective-permute-start.2 = (bf16[4,4,578]{2,1,0:T(4,128)(2,1)S(1)}, bf16[4,4,578]{2,1,0:T(4,128)(2,1)S(1)}, u32[]{:S(2)}, u32[]{:S(2)}) collective-permute-start(bf16[4,4,578]{2,1,0:T(4,128)(2,1)S(1)} %get-tuple-element.275), channel_id=1, source_target_pairs={{0,4},{4,8},{8,12},{12,16},{16,20},{20,24},{24,28},{28,32},{32,36}... | collective-permute-start | bytes 55496 | tf_op jit(solution)/shard_map/ppermute | solution.py:14
  20.3 4.5 %collective-permute-start.3 = (bf16[4,4,578]{2,1,0:T(4,128)(2,1)S(1)}, bf16[4,4,578]{2,1,0:T(4,128)(2,1)S(1)}, u32[]{:S(2)}, u32[]{:S(2)}) collective-permute-start(bf16[4,4,578]{2,1,0:T(4,128)(2,1)S(1)} %get-tuple-element.274), channel_id=1, source_target_pairs={{0,8},{4,12},{8,16},{12,20},{16,24},{20,28},{24,32},{28,36},{32,40... | collective-permute-start | bytes 55496 | tf_op jit(solution)/shard_map/ppermute | solution.py:14
  37.0 2.7 %copy-start.4 = (s32[1,1,8]{2,1,0:T(1,128)S(1)}, s32[1,1,8]{2,1,0:T(1,128)}, u32[]{:S(2)}) copy-start(s32[1,1,8]{2,1,0:T(1,128)} %param.24) | copy-start | bytes 100
  37.0 2.7 %copy-start.5 = (s32[1,1,8]{2,1,0:T(1,128)S(1)}, s32[1,1,8]{2,1,0:T(1,128)}, u32[]{:S(2)}) copy-start(s32[1,1,8]{2,1,0:T(1,128)} %param.23) | copy-start | bytes 100
  39.7 77.6 %copy-start.3 = (f32[3]{0:T(128)S(1)}, f32[3]{0:T(128)}, u32[]{:S(2)}) copy-start(f32[3]{0:T(128)} %param.19) | copy-start | bytes 40
  39.7 77.9 %copy-start.2 = (f32[4,578]{1,0:T(4,128)S(1)}, f32[4,578]{1,0:T(4,128)}, u32[]{:S(2)}) copy-start(f32[4,578]{1,0:T(4,128)} %param.18) | copy-start | bytes 27748
  117.7 35.7 %copy-start.1 = (f32[4,3,578]{2,0,1:T(4,128)}, f32[4,3,578]{2,0,1:T(4,128)S(1)}, u32[]{:S(2)}) copy-start(f32[4,3,578]{2,0,1:T(4,128)S(1)} %reshape.170) | copy-start | bytes 83236
  118.5 16.4 %collective-permute-start.4 = (bf16[4,3,578]{2,0,1:T(4,128)(2,1)S(1)}, bf16[4,3,578]{2,0,1:T(4,128)(2,1)S(1)}, u32[]{:S(2)}, u32[]{:S(2)}) collective-permute-start(bf16[4,3,578]{2,0,1:T(4,128)(2,1)S(1)} %get-tuple-element.282), channel_id=1, source_target_pairs={{8,0},{12,4},{16,8},{20,12},{24,16},{28,20},{32,24},{36,28},{40,32... | collective-permute-start | bytes 41624 | tf_op jit(solution)/shard_map/ppermute | solution.py:14
  120.4 20.9 %collective-permute-start.7 = (bf16[4,3,578]{2,0,1:T(4,128)(2,1)S(1)}, bf16[4,3,578]{2,0,1:T(4,128)(2,1)S(1)}, u32[]{:S(2)}, u32[]{:S(2)}) collective-permute-start(bf16[4,3,578]{2,0,1:T(4,128)(2,1)S(1)} %get-tuple-element.279), channel_id=1, source_target_pairs={{0,8},{4,12},{8,16},{12,20},{16,24},{20,28},{24,32},{28,36},{32,40... | collective-permute-start | bytes 41624 | tf_op jit(solution)/shard_map/ppermute | solution.py:14
  127.1 14.2 %collective-permute-start.6 = (bf16[4,3,578]{2,0,1:T(4,128)(2,1)S(1)}, bf16[4,3,578]{2,0,1:T(4,128)(2,1)S(1)}, u32[]{:S(2)}, u32[]{:S(2)}) collective-permute-start(bf16[4,3,578]{2,0,1:T(4,128)(2,1)S(1)} %get-tuple-element.280), channel_id=1, source_target_pairs={{0,4},{4,8},{8,12},{12,16},{16,20},{20,24},{24,28},{28,32},{32,36}... | collective-permute-start | bytes 41624 | tf_op jit(solution)/shard_map/ppermute | solution.py:14
  133.0 8.4 %collective-permute-start.5 = (bf16[4,3,578]{2,0,1:T(4,128)(2,1)S(1)}, bf16[4,3,578]{2,0,1:T(4,128)(2,1)S(1)}, u32[]{:S(2)}, u32[]{:S(2)}) collective-permute-start(bf16[4,3,578]{2,0,1:T(4,128)(2,1)S(1)} %get-tuple-element.281), channel_id=1, source_target_pairs={{4,0},{8,4},{12,8},{16,12},{20,16},{24,20},{28,24},{32,28},{36,32}... | collective-permute-start | bytes 41624 | tf_op jit(solution)/shard_map/ppermute | solution.py:14
where the time goes:
time: 254 us; the launch traced here: 250 us
  loops' own time  75.8 us (30%)
  other arithmetic  55.4 us (22%)
  local copies, waits for them, and re-layouts  53.8 us (21%)
  starting transfers between devices  27.4 us (11%)
  blocking collectives  20.4 us (8%)
  waiting for transfers between devices  12.6 us (5%)
  matrix products  3.66 us (1%)
    another operation x2, loops' own time, pair_loop(): return lax.fori_loop(0, loop_count, step, empty)  75.8 us
    ppermute x8, starting transfers between devices, shifted(): return lax.ppermute(x, axis, pairs)  27.4 us
    all_gather x2, blocking collectives, deliver(): grouped = lax.all_gather(received[None], 'tgt', axis=0, tiled=True)  20.4 us
    reduce_sum x8, other arithmetic, stokes_term(): return jnp.sum(first + second, axis=1) / (8.0 * math.pi)  15.7 us
    ppermute x8, waiting for transfers between devices, shifted(): return lax.ppermute(x, axis, pairs)  12.6 us
    reduce_sum x8, other arithmetic, stokes_term(): dist_sq = jnp.sum(apart * apart, axis=0) + reg_square  12.5 us
    dynamic_slice x16, local copies, waits for them, and re-layouts, step(): row_index = row_table[index]  9.91 us
    dynamic_slice x16, local copies, waits for them, and re-layouts, step(): tile_index = tile_table[index]  9.88 us
  transfers between devices with their start and end apart: 8, of which 3 were waited for; matrix products, arithmetic and copies ran while one was open for 1% of the time, Pallas kernels for 0%

commit v1 on v0

v1 whole, which is shorter than its diff:
```python
import functools
import math

import jax
import jax.numpy as jnp
from jax import lax
from jax.experimental import pallas as pl
from jax.experimental.pallas import tpu as pltpu
from jax.sharding import Mesh
from jax.sharding import PartitionSpec as P

REG = 0.25
VMEM = pl.BlockSpec(memory_space=pltpu.VMEM)
SMEM = pl.BlockSpec(memory_space=pltpu.SMEM)


def ceil_to(n, m):
    return -(-n // m) * m


def iota(shape, dim):
    return lax.broadcasted_iota(jnp.int32, shape, dim)


def split3(x):
    high = x.astype(jnp.bfloat16).astype(jnp.float32)
    rest = x - high
    mid = rest.astype(jnp.bfloat16).astype(jnp.float32)
    low = (rest - mid).astype(jnp.bfloat16).astype(jnp.float32)
    return high, mid, low


def pack_kernel(nodes, send_ref, pos_ref, charge_ref, weight_ref, out_ref, block):
    drops = pos_ref.shape[0]
    lanes = block.shape[1]
    block[...] = jnp.zeros_like(block)
    for d in range(drops):
        block[d * 4 : d * 4 + 3, 0:nodes] = pos_ref[d]
        block[d * 4 + 3 : d * 4 + 4, 0:nodes] = (
            charge_ref[d : d + 1, :] * weight_ref[d : d + 1, :]
        )
    base = nodes - (lanes - 128)
    lane = iota((1, 128), 1)
    row = block[0:1, lanes - 128 : lanes]
    shell, slots = send_ref.shape
    for o in range(shell):
        for j in range(slots):
            row = jnp.where(
                lane == base + o * slots + j, send_ref[o, j].astype(jnp.float32), row
            )
    block[0:1, lanes - 128 : lanes] = row
    packed = block[...].astype(jnp.bfloat16)
    for i in range(out_ref.shape[0]):
        out_ref[i] = packed


def fetch_blocks(slot_ref, below_ref, own_ref, above_ref, rows):
    core = lax.axis_index("core")
    pairs = slot_ref.shape[0]
    for k in range(pairs):
        p = slot_ref[k]
        owner = p // 20
        place = core + 4 - (p // 4) % 5
        chip = place // 2
        index = (place % 2) * 4 + owner
        for which, ref in enumerate((below_ref, own_ref, above_ref)):

            @pl.when(chip == which)
            def _(ref=ref, k=k, index=index):
                rows[k * 16 : (k + 1) * 16, :] = ref[index]


def tile_slices(nodes):
    half = nodes // 2
    return [(0, half), (half, nodes)]


def centred(pos, half, height):
    mean = jnp.sum(pos, axis=1, keepdims=True) / half
    return pos - mean, mean


def field_kernel(
    nodes,
    slot_ref,
    tile_ref,
    count_ref,
    applied_ref,
    below_ref,
    own_ref,
    above_ref,
    up_ref,
    pos_ref,
    normal_ref,
    weight_ref,
    trac_ref,
    send_ref,
    cube_ref,
    hot_ref,
    fine_ref,
    rows,
    block,
    targets,
    means,
    feats,
    near,
):
    pairs = slot_ref.shape[0]
    drops = pos_ref.shape[0]
    half = nodes // 2
    wide = feats.shape[1]
    lanes = rows.shape[1]
    fine_nodes = up_ref.shape[1]

    fetch_blocks(slot_ref, below_ref, own_ref, above_ref, rows)
    height = pairs * 8
    base = nodes - (lanes - 128)
    row_id = iota((height, 128), 0)
    lane_id = iota((height, 128), 1)
    want = jnp.zeros((height, 128), jnp.int32)
    table = []
    for k in range(pairs):
        want = jnp.where(row_id // 8 == k, base + slot_ref[k] % 20, want)
        head = rows[k * 16 : (k + 1) * 16, lanes - 128 : lanes].astype(jnp.float32)[0:1]
        table.append(jnp.broadcast_to(head, (8, 128)))
    table = jnp.concatenate(table, axis=0)
    chosen = jnp.sum(jnp.where(lane_id == want, table, 0.0), axis=1, keepdims=True)
    column = (row_id // 8) * 16 + row_id % 4 + 4 * chosen.astype(jnp.int32)
    hot = (lane_id == column).astype(jnp.float32).astype(jnp.bfloat16)
    hot_ref[...] = hot
    picked = jnp.dot(hot, rows[...], preferred_element_type=jnp.float32)
    fine = jnp.dot(
        picked[:, 0:nodes].astype(jnp.bfloat16),
        up_ref[...],
        preferred_element_type=jnp.float32,
    )
    for k in range(pairs):
        fine_ref[k] = fine[k * 8 : (k + 1) * 8]

    near[...] = jnp.zeros_like(near)
    targets[...] = jnp.zeros_like(targets)
    for d in range(drops):
        for h, (lo, hi) in enumerate(tile_slices(nodes)):
            b = d * 2 + h
            pos, mean = centred(pos_ref[d, :, lo:hi], half, 8)
            targets[b, 0:3, 0:half] = pos
            means[b, 0:3, :] = jnp.broadcast_to(mean, (3, 128))
            means[b, 3:8, :] = jnp.zeros((5, 128), jnp.float32)
    sub = iota((8, wide), 0)
    for b in range(2 * drops):
        t = targets[b]
        norm = jnp.sum(t * t, axis=0, keepdims=True)
        t8 = jnp.where(sub < 4, t, jnp.concatenate([t[4:8], t[0:4]], axis=0))
        t8 = jnp.where(sub % 4 == 3, 1.0, t8)
        high, mid, low = split3(t8)
        nh, nm, nl = split3(norm)
        last = jnp.where(
            sub == 0, nh, jnp.where(sub == 1, nm, jnp.where(sub == 2, nl, 0.0))
        )
        stack = jnp.concatenate([high, mid, jnp.where(sub < 4, high, low), last], axis=0)
        feats[b] = stack.T.astype(jnp.bfloat16)

    sub_f = iota((8, fine_nodes), 0)

    def pair(k, carry):
        b = tile_ref[k]
        f = fine_ref[k]
        m = means[b, :, 0:1]
        m8 = jnp.where(iota((8, 1), 0) < 4, m, jnp.concatenate([m[4:8], m[0:4]], axis=0))
        charge = f[3:4]
        y = f - m8
        y_only = jnp.where(sub_f < 3, y, 0.0)
        norm = jnp.sum(y_only * y_only, axis=0, keepdims=True) + REG
        q = jnp.where(sub_f % 4 == 3, norm, -2.0 * y)
        high, mid, low = split3(q)
        first = jnp.where(sub_f < 4, high, mid)
        second = jnp.where(sub_f < 4, low, high)
        third = jnp.where(sub_f < 3, 1.0, 0.0)
        src = jnp.concatenate([first, first, second, third], axis=0).astype(jnp.bfloat16)
        coef = jnp.where(sub_f % 4 == 3, charge, charge * y)
        high, mid, low = split3(coef)
        coefs = jnp.concatenate(
            [jnp.where(sub_f < 4, high, mid), jnp.where(sub_f < 4, low, 0.0)], axis=0
        ).astype(jnp.bfloat16)
        tgt = feats[b]
        total = jnp.zeros((wide, 16), jnp.float32)
        for lo in range(0, fine_nodes, 256):
            hi = min(lo + 256, fine_nodes)
            dist = jnp.dot(tgt, src[:, lo:hi], preferred_element_type=jnp.float32)
            inv = lax.rsqrt(jnp.maximum(dist, REG))
            cube = (inv * inv * inv).astype(jnp.bfloat16)
            cube_ref[k, :, lo:hi] = cube
            total = total + lax.dot_general(
                cube,
                coefs[:, lo:hi],
                (((1,), (1,)), ((), ())),
                preferred_element_type=jnp.float32,
            )
        sums = total.T
        sums = sums[0:8] + sums[8:16]
        sums = sums + jnp.concatenate([sums[4:8], sums[0:4]], axis=0)
        near[b] += (targets[b] * sums[3:4] - sums) * (1.0 / (4.0 * math.pi))
        return carry

    lax.fori_loop(0, count_ref[0], pair, 0)

    block[...] = jnp.zeros_like(block)
    for d in range(drops):
        for h, (lo, hi) in enumerate(tile_slices(nodes)):
            e = near[d * 2 + h][0:3, 0:half]
            part = []
            for c in range(3):
                part.append(e[c : c + 1] + applied_ref[c])
            e = jnp.concatenate(part, axis=0)
            n = normal_ref[d, :, lo:hi]
            along = jnp.sum(e * n, axis=0, keepdims=True)
            square = jnp.sum(e * e, axis=0, keepdims=True)
            t = along * e - 0.5 * square * n
            trac_ref[d, :, lo:hi] = t
            block[d * 4 : d * 4 + 3, lo:hi] = t * weight_ref[d : d + 1, lo:hi]
    packed = block[...].astype(jnp.bfloat16)
    for i in range(send_ref.shape[0]):
        send_ref[i] = packed


def stokes_kernel(
    nodes,
    slot_ref,
    tile_ref,
    count_ref,
    below_ref,
    own_ref,
    above_ref,
    up_ref,
    pos_ref,
    cube_ref,
    hot_ref,
    fine_ref,
    vel_ref,
    rows,
    targets,
    means,
    forces,
    flow,
):
    pairs = slot_ref.shape[0]
    drops = pos_ref.shape[0]
    half = nodes // 2
    fine_nodes = up_ref.shape[1]
    wide = targets.shape[2]

    fetch_blocks(slot_ref, below_ref, own_ref, above_ref, rows)
    picked = jnp.dot(hot_ref[...], rows[...], preferred_element_type=jnp.float32)
    fine = jnp.dot(
        picked[:, 0:nodes].astype(jnp.bfloat16),
        up_ref[...],
        preferred_element_type=jnp.float32,
    )
    for k in range(pairs):
        forces[k] = fine[k * 8 : (k + 1) * 8]

    flow[...] = jnp.zeros_like(flow)
    targets[...] = jnp.zeros_like(targets)
    for d in range(drops):
        for h, (lo, hi) in enumerate(tile_slices(nodes)):
            b = d * 2 + h
            pos, mean = centred(pos_ref[d, :, lo:hi], half, 8)
            targets[b, 0:3, 0:half] = pos
            means[b, 0:3, :] = jnp.broadcast_to(mean, (3, 128))
            means[b, 3:8, :] = jnp.zeros((5, 128), jnp.float32)

    sub_f = iota((8, fine_nodes), 0)

    def pair(k, carry):
        b = tile_ref[k]
        m = means[b, :, 0:1]
        m8 = jnp.where(iota((8, 1), 0) < 4, m, jnp.concatenate([m[4:8], m[0:4]], axis=0))
        y = fine_ref[k] - m8
        f = forces[k]
        y_only = jnp.where(sub_f < 3, y, 0.0)
        norm = jnp.sum(y_only * y_only, axis=0, keepdims=True)
        dot = jnp.sum(y_only * f, axis=0, keepdims=True)
        one = f * jnp.where(sub_f < 4, 1.0, norm)
        two = f * jnp.where(sub_f < 4, y[0:1], y[1:2])
        three = jnp.where(sub_f < 4, f * y[2:3], dot * y)
        parts = [split3(one), split3(two), split3(three)]
        coefs = jnp.concatenate(
            [parts[g][s] for s in range(3) for g in range(3)]
            + [jnp.zeros((8, fine_nodes), jnp.float32)],
            axis=0,
        ).astype(jnp.bfloat16)
        total = jnp.zeros((wide, 80), jnp.float32)
        for lo in range(0, fine_nodes, 256):
            hi = min(lo + 256, fine_nodes)
            total = total + lax.dot_general(
                cube_ref[k, :, lo:hi],
                coefs[:, lo:hi],
                (((1,), (1,)), ((), ())),
                preferred_element_type=jnp.float32,
            )
        sums = total.T
        sums = sums[0:24] + sums[24:48] + sums[48:72]
        x = targets[b][0:3]
        force, force_sq = sums[0:3], sums[4:7]
        t0, t1, t2 = sums[8:11], sums[12:15], sums[16:19]
        last = sums[20:23]
        x0, x1, x2 = x[0:1], x[1:2], x[2:3]
        square = x0 * x0 + x1 * x1 + x2 * x2
        trace = t0[0:1] + t1[1:2] + t2[2:3]
        reach = jnp.sum(x * force, axis=0, keepdims=True) - trace
        mixed = jnp.concatenate(
            [jnp.sum(x * t, axis=0, keepdims=True) for t in (t0, t1, t2)], axis=0
        )
        v = (square + 2.0 * REG) * force + force_sq
        v = v - 2.0 * (x0 * t0 + x1 * t1 + x2 * t2) + x * reach - mixed + last
        flow[b, 0:3, :] += v * (1.0 / (8.0 * math.pi))
        return carry

    lax.fori_loop(0, count_ref[0], pair, 0)
    for d in range(drops):
        for h, (lo, hi) in enumerate(tile_slices(nodes)):
            vel_ref[d, :, lo:hi] = flow[d * 2 + h][0:3, 0:half]


def exchange(mine, chips):
    own = lax.all_to_all(mine, ("core", "tgt"), 0, 0)
    below = lax.ppermute(own, "chip", [(i, i + 1) for i in range(chips - 1)])
    above = lax.ppermute(own, "chip", [(i + 1, i) for i in range(chips - 1)])
    return below, own, above


def local(
    chips,
    positions,
    normals,
    charge,
    weights,
    applied,
    upsample,
    send_list,
    send_count,
    pair_slot,
    pair_tile,
    pair_count,
):
    drops, _, nodes = positions.shape
    fine_nodes = upsample.shape[1]
    pairs = pair_slot.shape[2]
    lanes = ceil_to(nodes + 20, 128)
    wide = ceil_to(nodes // 2, 16)
    tiles = 2 * drops
    f32, bf16 = jnp.float32, jnp.bfloat16
    slots, tile_ids, count = pair_slot[0, 0], pair_tile[0, 0], pair_count[0]

    mine = pl.pallas_call(
        functools.partial(pack_kernel, nodes),
        out_shape=jax.ShapeDtypeStruct((8, 16, lanes), bf16),
        in_specs=[SMEM, VMEM, VMEM, VMEM],
        out_specs=VMEM,
        scratch_shapes=[pltpu.VMEM((16, lanes), f32)],
        name="pack",
    )(send_list[0, 0], positions, charge, weights)
    gathered = exchange(mine, chips)

    traction, forces, cubes, hot, fine = pl.pallas_call(
        functools.partial(field_kernel, nodes),
        out_shape=(
            jax.ShapeDtypeStruct((drops, 3, nodes), f32),
            jax.ShapeDtypeStruct((8, 16, lanes), bf16),
            jax.ShapeDtypeStruct((pairs, wide, fine_nodes), bf16),
            jax.ShapeDtypeStruct((pairs * 8, 128), bf16),
            jax.ShapeDtypeStruct((pairs, 8, fine_nodes), f32),
        ),
        in_specs=[SMEM] * 4 + [VMEM] * 7,
        out_specs=(VMEM,) * 5,
        scratch_shapes=[
            pltpu.VMEM((pairs * 16, lanes), bf16),
            pltpu.VMEM((16, lanes), f32),
            pltpu.VMEM((tiles, 8, wide), f32),
            pltpu.VMEM((tiles, 8, 128), f32),
            pltpu.VMEM((tiles, wide, 32), bf16),
            pltpu.VMEM((tiles, 8, wide), f32),
        ],
        name="field",
    )(slots, tile_ids, count, applied, *gathered, upsample, positions, normals, weights)
    gathered = exchange(forces, chips)

    velocity = pl.pallas_call(
        functools.partial(stokes_kernel, nodes),
        out_shape=jax.ShapeDtypeStruct((drops, 3, nodes), f32),
        in_specs=[SMEM] * 3 + [VMEM] * 8,
        out_specs=VMEM,
        scratch_shapes=[
            pltpu.VMEM((pairs * 16, lanes), bf16),
            pltpu.VMEM((tiles, 8, wide), f32),
            pltpu.VMEM((tiles, 8, 128), f32),
            pltpu.VMEM((pairs, 8, fine_nodes), f32),
            pltpu.VMEM((tiles, 8, wide), f32),
        ],
        name="stokes",
    )(slots, tile_ids, count, *gathered, upsample, positions, cubes, hot, fine)
    return traction, velocity


def solution(mesh):
    space, tgt = mesh.shape["space"], mesh.shape["tgt"]
    chips = space // 2
    fine_mesh = Mesh(mesh.devices.reshape(chips, 2, tgt), ("chip", "core", "tgt"))
    every = ("chip", "core", "tgt")
    rows = ("chip", "core")
    placed = (
        P(every, None, None),
        P(every, None, None),
        P(every, None),
        P(every, None),
        P(),
        P(),
        P(rows, "tgt", None, None),
        P(rows, "tgt", None),
        P(rows, "tgt", None),
        P(rows, "tgt", None),
        P(rows, "tgt"),
    )
    return jax.shard_map(
        functools.partial(local, chips),
        mesh=fine_mesh,
        in_specs=placed,
        out_specs=(P(every, None, None), P(every, None, None)),
        check_vma=False,
    )
```

time: 254 us -> 86.7 us (0.34)
  the two profiles are of different devices: /device:TPU:103 before, /device:TPU:385 now
where the time goes in v1:
time: 86.7 us; the launch traced here: 85.9 us
  Pallas kernels  31 us (36%)
  blocking collectives  20 us (23%)
  starting transfers between devices  13.2 us (15%)
  waiting for transfers between devices  12.2 us (14%)
  local copies, waits for them, and re-layouts  8.22 us (9%)
  between operations  1.32 us (2%)
    all_to_all x2, blocking collectives, exchange(): own = lax.all_to_all(mine, ('core', 'tgt'), 0, 0)  20 us
    pallas_call x1, Pallas kernels, local(): pl.pallas_call(functools.partial(field_kernel, nodes), out_shape=(jax.Sha...  17.1 us
    pallas_call x1, Pallas kernels, local(): pl.pallas_call(functools.partial(stokes_kernel, nodes), out_shape=jax.Sha...  12.4 us
    ppermute x2, waiting for transfers between devices, exchange(): below = lax.ppermute(own, 'chip', [(i, i + 1) for i in range(chips - 1)])  11.5 us
    ppermute x2, starting transfers between devices, exchange(): above = lax.ppermute(own, 'chip', [(i + 1, i) for i in range(chips - 1)])  7.97 us
    unnamed x16, local copies, waits for them, and re-layouts  6.86 us
    ppermute x2, starting transfers between devices, exchange(): below = lax.ppermute(own, 'chip', [(i, i + 1) for i in range(chips - 1)])  5.25 us
  transfers between devices with their start and end apart: 4, of which 3 were waited for; matrix products, arithmetic and copies ran while one was open for 3% of the time, Pallas kernels for 0%

profile of v1, /device:TPU:385, one launch (start us, length us, event | category | flops | bytes accessed | tf_op | source)
XLA Modules:
  0.0 85.9 jit_solution(12141538940781843010)
XLA Ops:
  0.6 1.4 %copy.12.send_ref = s32[5,4]{1,0:T(8,128)} copy(s32[5,4]{0,1:T(4,128)} %bitcast.6) | data formatting | bytes 160 | tf_op jit(solution)/shard_map/squeeze | solution.py:362
  2.0 1.4 %copy.13.pos_ref = f32[4,3,578]{2,1,0:T(4,128)} copy(f32[4,3,578]{2,0,1:T(4,128)} %param.11) | data formatting | bytes 55488 | tf_op args[0]
  3.4 1.6 %pack.1 = bf16[8,16,640]{2,1,0:T(8,128)(2,1)} custom-call(s32[5,4]{1,0:T(8,128)} %copy.12.send_ref, f32[4,3,578]{2,1,0:T(4,128)} %copy.13.pos_ref, f32[4,578]{1,0:T(4,128)} %charge_ref.1, f32[4,578]{1,0:T(4,128)} %weight_ref.3), custom_call_target="tpu_custom_call" | custom-call | tf_op jit(solution)/shard_map/pack/pallas_call | solution.py:355
  4.9 10.6 %all_to_all.10.own_ref = bf16[8,16,640]{2,1,0:T(8,128)(2,1)S(1)} all-to-all(bf16[8,16,640]{2,1,0:T(8,128)(2,1)} %pack.1), channel_id=1, replica_groups=mesh['chip'=64,'core'=2,'tgt'=4] {'core','tgt'}, dimensions={0} | all-to-all | bytes 327680 | tf_op jit(solution)/shard_map/all_to_all | solution.py:326
  15.5 6.0 %collective-permute-start.1 = (bf16[8,16,640]{2,1,0:T(8,128)(2,1)S(1)}, bf16[8,16,640]{2,1,0:T(8,128)(2,1)S(1)}, u32[]{:S(2)}, u32[]{:S(2)}) collective-permute-start(bf16[8,16,640]{2,1,0:T(8,128)(2,1)S(1)} %all_to_all.10.own_ref), channel_id=1, source_target_pairs={{8,0},{16,8},{24,16},{32,24},{40,32},{48,40},{56,48},{64,56},{72,6... | collective-permute-start | bytes 491528 | tf_op jit(solution)/shard_map/ppermute | solution.py:328
  21.6 1.9 %collective-permute-start = (bf16[8,16,640]{2,1,0:T(8,128)(2,1)S(1)}, bf16[8,16,640]{2,1,0:T(8,128)(2,1)S(1)}, u32[]{:S(2)}, u32[]{:S(2)}) collective-permute-start(bf16[8,16,640]{2,1,0:T(8,128)(2,1)S(1)} %all_to_all.10.own_ref), channel_id=1, source_target_pairs={{0,8},{8,16},{16,24},{24,32},{32,40},{40,48},{48,56},{56,64},{64,7... | collective-permute-start | bytes 491528 | tf_op jit(solution)/shard_map/ppermute | solution.py:327
  24.1 1.4 %copy.15.normal_ref = f32[4,3,578]{2,1,0:T(4,128)} copy(f32[4,3,578]{2,0,1:T(4,128)} %param.12) | data formatting | bytes 55488 | tf_op args[1]
  25.5 0.0 collective-permute-done.1.above_ref
  25.5 6.5 %collective-permute-done.below_ref = bf16[8,16,640]{2,1,0:T(8,128)(2,1)S(1)} collective-permute-done((bf16[8,16,640]{2,1,0:T(8,128)(2,1)S(1)}, bf16[8,16,640]{2,1,0:T(8,128)(2,1)S(1)}, u32[]{:S(2)}, u32[]{:S(2)}) %collective-permute-start) | collective-permute-done | bytes 163872 | tf_op jit(solution)/shard_map/ppermute | solution.py:327
  32.0 0.0 copy-done.1
  32.0 0.0 copy-done.4
  32.0 0.6 copy-done.5
  32.7 17.1 %field.1 = (f32[4,3,578]{2,1,0:T(4,128)}, bf16[8,16,640]{2,1,0:T(8,128)(2,1)}, bf16[8,304,2112]{2,1,0:T(8,128)(2,1)}, bf16[64,128]{1,0:T(8,128)(2,1)}, f32[8,8,2112]{2,1,0:T(8,128)}) custom-call(s32[8]{0:T(128)} %bitcast.7, s32[8]{0:T(128)} %bitcast.9, s32[1]{0:T(128)} %bitcast.4.count_ref, f32[3]{0:T(128)} %applied_ref.1, bf16[8,16,640]{2,1,0:T(8,128)(2,1)} %copy-done.5, ...), custom_call_target="tpu_custom_call" | custom-call | tf_op jit(solution)/shard_map/field/pallas_call | solution.py:365
  49.7 9.4 %all_to_all.11.own_ref = bf16[8,16,640]{2,1,0:T(8,128)(2,1)S(1)} all-to-all(bf16[8,16,640]{2,1,0:T(8,128)(2,1)} %get-tuple-element.8), channel_id=1, replica_groups=mesh['chip'=64,'core'=2,'tgt'=4] {'core','tgt'}, dimensions={0} | all-to-all | bytes 327680 | tf_op jit(solution)/shard_map/all_to_all | solution.py:326
  59.1 1.9 %collective-permute-start.3 = (bf16[8,16,640]{2,1,0:T(8,128)(2,1)S(1)}, bf16[8,16,640]{2,1,0:T(8,128)(2,1)S(1)}, u32[]{:S(2)}, u32[]{:S(2)}) collective-permute-start(bf16[8,16,640]{2,1,0:T(8,128)(2,1)S(1)} %all_to_all.11.own_ref), channel_id=1, source_target_pairs={{8,0},{16,8},{24,16},{32,24},{40,32},{48,40},{56,48},{64,56},{72,6... | collective-permute-start | bytes 491528 | tf_op jit(solution)/shard_map/ppermute | solution.py:328
  61.1 3.3 %collective-permute-start.2 = (bf16[8,16,640]{2,1,0:T(8,128)(2,1)S(1)}, bf16[8,16,640]{2,1,0:T(8,128)(2,1)S(1)}, u32[]{:S(2)}, u32[]{:S(2)}) collective-permute-start(bf16[8,16,640]{2,1,0:T(8,128)(2,1)S(1)} %all_to_all.11.own_ref), channel_id=1, source_target_pairs={{0,8},{8,16},{16,24},{24,32},{32,40},{40,48},{48,56},{56,64},{64,7... | collective-permute-start | bytes 491528 | tf_op jit(solution)/shard_map/ppermute | solution.py:327
  64.4 1.4 %copy.17 = f32[4,3,578]{2,0,1:T(4,128)} copy(f32[4,3,578]{2,1,0:T(4,128)} %get-tuple-element.12) | data formatting | bytes 55488
  65.8 0.7 collective-permute-done.3.above_ref
  66.5 5.0 %collective-permute-done.2.below_ref = bf16[8,16,640]{2,1,0:T(8,128)(2,1)S(1)} collective-permute-done((bf16[8,16,640]{2,1,0:T(8,128)(2,1)S(1)}, bf16[8,16,640]{2,1,0:T(8,128)(2,1)S(1)}, u32[]{:S(2)}, u32[]{:S(2)}) %collective-permute-start.2) | collective-permute-done | bytes 163872 | tf_op jit(solution)/shard_map/ppermute | solution.py:327
  71.5 0.0 copy-done
  71.5 0.0 copy-done.2
  71.5 0.6 copy-done.3
  72.1 12.4 %stokes.1 = f32[4,3,578]{2,1,0:T(4,128)} custom-call(s32[8]{0:T(128)} %bitcast.8, s32[8]{0:T(128)} %bitcast.10, s32[1]{0:T(128)} %bitcast.5.count_ref, bf16[8,16,640]{2,1,0:T(8,128)(2,1)} %copy-done.3, bf16[8,16,640]{2,1,0:T(8,128)(2,1)} %copy-done, bf16[8,16,640]{2,1,0:T(8,128)(2,1)} %copy-done.2, bf16[578,2112]{1,0:T(8,128)(2,1)} %up_ref.3, ...), custom_call_target="tpu_custom_call" | custom-call | tf_op jit(solution)/shard_map/stokes/pallas_call | solution.py:388
  84.5 1.4 %copy.18 = f32[4,3,578]{2,0,1:T(4,128)} copy(f32[4,3,578]{2,1,0:T(4,128)} %stokes.1) | data formatting | bytes 55488
  (6 shorter events, 0.0 us)
Async XLA Ops:
  15.5 16.5 %copy-start.1 = (bf16[8,16,640]{2,1,0:T(8,128)(2,1)}, bf16[8,16,640]{2,1,0:T(8,128)(2,1)S(1)}, u32[]{:S(2)}) copy-start(bf16[8,16,640]{2,1,0:T(8,128)(2,1)S(1)} %all_to_all.10.own_ref) | copy-start | bytes 491524
  15.5 10.0 %collective-permute-start.1 = (bf16[8,16,640]{2,1,0:T(8,128)(2,1)S(1)}, bf16[8,16,640]{2,1,0:T(8,128)(2,1)S(1)}, u32[]{:S(2)}, u32[]{:S(2)}) collective-permute-start(bf16[8,16,640]{2,1,0:T(8,128)(2,1)S(1)} %all_to_all.10.own_ref), channel_id=1, source_target_pairs={{8,0},{16,8},{24,16},{32,24},{40,32},{48,40},{56,48},{64,56},{72,6... | collective-permute-start | bytes 491528 | tf_op jit(solution)/shard_map/ppermute | solution.py:328
  21.6 10.4 %collective-permute-start = (bf16[8,16,640]{2,1,0:T(8,128)(2,1)S(1)}, bf16[8,16,640]{2,1,0:T(8,128)(2,1)S(1)}, u32[]{:S(2)}, u32[]{:S(2)}) collective-permute-start(bf16[8,16,640]{2,1,0:T(8,128)(2,1)S(1)} %all_to_all.10.own_ref), channel_id=1, source_target_pairs={{0,8},{8,16},{16,24},{24,32},{32,40},{40,48},{48,56},{56,64},{64,7... | collective-permute-start | bytes 491528 | tf_op jit(solution)/shard_map/ppermute | solution.py:327
  25.5 6.5 %copy-start.4 = (bf16[8,16,640]{2,1,0:T(8,128)(2,1)}, bf16[8,16,640]{2,1,0:T(8,128)(2,1)S(1)}, u32[]{:S(2)}) copy-start(bf16[8,16,640]{2,1,0:T(8,128)(2,1)S(1)} %collective-permute-done.1.above_ref) | copy-start | bytes 491524
  32.0 0.7 copy-start.5
  59.1 12.4 %copy-start = (bf16[8,16,640]{2,1,0:T(8,128)(2,1)}, bf16[8,16,640]{2,1,0:T(8,128)(2,1)S(1)}, u32[]{:S(2)}) copy-start(bf16[8,16,640]{2,1,0:T(8,128)(2,1)S(1)} %all_to_all.11.own_ref) | copy-start | bytes 491524
  59.1 7.4 %collective-permute-start.3 = (bf16[8,16,640]{2,1,0:T(8,128)(2,1)S(1)}, bf16[8,16,640]{2,1,0:T(8,128)(2,1)S(1)}, u32[]{:S(2)}, u32[]{:S(2)}) collective-permute-start(bf16[8,16,640]{2,1,0:T(8,128)(2,1)S(1)} %all_to_all.11.own_ref), channel_id=1, source_target_pairs={{8,0},{16,8},{24,16},{32,24},{40,32},{48,40},{56,48},{64,56},{72,6... | collective-permute-start | bytes 491528 | tf_op jit(solution)/shard_map/ppermute | solution.py:328
  61.1 10.4 %collective-permute-start.2 = (bf16[8,16,640]{2,1,0:T(8,128)(2,1)S(1)}, bf16[8,16,640]{2,1,0:T(8,128)(2,1)S(1)}, u32[]{:S(2)}, u32[]{:S(2)}) collective-permute-start(bf16[8,16,640]{2,1,0:T(8,128)(2,1)S(1)} %all_to_all.11.own_ref), channel_id=1, source_target_pairs={{0,8},{8,16},{16,24},{24,32},{32,40},{40,48},{48,56},{56,64},{64,7... | collective-permute-start | bytes 491528 | tf_op jit(solution)/shard_map/ppermute | solution.py:327
  66.5 5.0 %copy-start.2 = (bf16[8,16,640]{2,1,0:T(8,128)(2,1)}, bf16[8,16,640]{2,1,0:T(8,128)(2,1)S(1)}, u32[]{:S(2)}) copy-start(bf16[8,16,640]{2,1,0:T(8,128)(2,1)S(1)} %collective-permute-done.3.above_ref) | copy-start | bytes 491524
  71.5 0.7 copy-start.3

commit v2 on v1

v2 whole, which is shorter than its diff:
```python
import functools
import math

import jax
import jax.numpy as jnp
from jax import lax
from jax.experimental import pallas as pl
from jax.experimental.pallas import tpu as pltpu
from jax.sharding import Mesh
from jax.sharding import PartitionSpec as P

REG = 0.25
VMEM = pl.BlockSpec(memory_space=pltpu.VMEM)
HBM = pl.BlockSpec(memory_space=pltpu.HBM)
SMEM = pl.BlockSpec(memory_space=pltpu.SMEM)
LIMIT = (2 << 20, 20 << 20, 20 << 20)


def ceil_to(n, m):
    return -(-n // m) * m


def iota(shape, dim):
    return lax.broadcasted_iota(jnp.int32, shape, dim)


def split3(x):
    high = x.astype(jnp.bfloat16).astype(jnp.float32)
    rest = x - high
    mid = rest.astype(jnp.bfloat16).astype(jnp.float32)
    low = (rest - mid).astype(jnp.bfloat16).astype(jnp.float32)
    return high, mid, low


def fetch_all(pairs, sems):
    copies = [
        pltpu.make_async_copy(src, dst, sems.at[i]) for i, (src, dst) in enumerate(pairs)
    ]
    for copy in copies:
        copy.start()
    return copies


def pack_kernel(
    nodes, send_hbm, pos_hbm, charge_hbm, weight_hbm, out_ref,
    send_ref, pos_ref, charge_ref, weight_ref, block, sems,
):
    copies = fetch_all(
        [
            (send_hbm, send_ref),
            (pos_hbm, pos_ref),
            (charge_hbm, charge_ref),
            (weight_hbm, weight_ref),
        ],
        sems,
    )
    lanes = block.shape[1]
    block[...] = jnp.zeros_like(block)
    for copy in copies:
        copy.wait()
    for c in range(3):
        block[c * 4 : (c + 1) * 4, 0:nodes] = pos_ref[c]
    block[12:16, 0:nodes] = charge_ref[...] * weight_ref[...]
    base = nodes - (lanes - 128)
    lane = iota((1, 128), 1)
    row = block[0:1, lanes - 128 : lanes]
    slots, shell = send_ref.shape
    for o in range(shell):
        for j in range(slots):
            row = jnp.where(
                lane == base + o * slots + j, send_ref[j, o].astype(jnp.float32), row
            )
    block[0:1, lanes - 128 : lanes] = row
    packed = block[...].astype(jnp.bfloat16)
    for i in range(out_ref.shape[0]):
        out_ref[i] = packed


def fetch_blocks(slot_ref, own_ref, side_ref, rows):
    core = lax.axis_index("core")
    for k in range(slot_ref.shape[1]):
        p = slot_ref[0, k]
        owner = p // 20
        place = core + 4 - (p // 4) % 5
        chip = place // 2
        index = (place % 2) * 4 + owner
        for which, ref in enumerate((side_ref.at[0], own_ref, side_ref.at[1])):

            @pl.when(chip == which)
            def _(ref=ref, k=k, index=index):
                rows[k * 16 : (k + 1) * 16, :] = ref[index]


def tile_slices(nodes):
    half = nodes // 2
    return [(0, half), (half, nodes)]


def target_kernel(pos_hbm, up_hbm, feat_ref, target_ref, mean_ref, up_ref, pos_ref, sems):
    copies = fetch_all([(pos_hbm, pos_ref), (up_hbm, up_ref)], sems)
    copies[0].wait()
    drops, nodes = pos_ref.shape[1:]
    half = nodes // 2
    wide = feat_ref.shape[1]
    target_ref[...] = jnp.zeros_like(target_ref)
    mean_ref[...] = jnp.zeros_like(mean_ref)
    for d in range(drops):
        for h, (lo, hi) in enumerate(tile_slices(nodes)):
            for c in range(3):
                row = pos_ref[c, d : d + 1, lo:hi]
                mean = jnp.sum(row, axis=1, keepdims=True) / half
                target_ref[d * 2 + h, c : c + 1, 0:half] = row - mean
                mean_ref[d * 2 + h, c : c + 1, :] = jnp.broadcast_to(mean, (1, 128))
                mean_ref[d * 2 + h, c + 4 : c + 5, :] = jnp.broadcast_to(mean, (1, 128))
    sub = iota((8, wide), 0)
    for b in range(2 * drops):
        t = target_ref[b]
        norm = jnp.sum(t * t, axis=0, keepdims=True)
        t8 = jnp.where(sub < 4, t, jnp.concatenate([t[4:8], t[0:4]], axis=0))
        t8 = jnp.where(sub % 4 == 3, 1.0, t8)
        high, mid, low = split3(t8)
        nh, nm, nl = split3(norm)
        last = jnp.where(
            sub == 0, nh, jnp.where(sub == 1, nm, jnp.where(sub == 2, nl, 0.0))
        )
        stack = jnp.concatenate([high, mid, jnp.where(sub < 4, high, low), last], axis=0)
        feat_ref[b] = stack.T.astype(jnp.bfloat16)
    copies[1].wait()


def field_kernel(
    nodes,
    count_ref,
    slot_hbm,
    tile_hbm,
    applied_hbm,
    normal_hbm,
    weight_hbm,
    own_ref,
    side_ref,
    up_ref,
    feats,
    targets,
    means,
    trac_ref,
    send_ref,
    cube_ref,
    hot_ref,
    fine_ref,
    slot_ref,
    tile_ref,
    applied_ref,
    normal_ref,
    weight_ref,
    rows,
    block,
    near,
    field,
    src_a,
    src_b,
    coef_a,
    coef_b,
    sems,
):
    copies = fetch_all(
        [
            (slot_hbm, slot_ref),
            (tile_hbm, tile_ref),
            (applied_hbm, applied_ref),
            (normal_hbm, normal_ref),
            (weight_hbm, weight_ref),
        ],
        sems,
    )
    pairs = slot_ref.shape[1]
    drops = weight_ref.shape[0]
    half = nodes // 2
    wide = feats.shape[1]
    lanes = rows.shape[1]
    fine_nodes = up_ref.shape[1]
    near[...] = jnp.zeros_like(near)
    block[...] = jnp.zeros_like(block)
    for copy in copies[:3]:
        copy.wait()

    fetch_blocks(slot_ref, own_ref, side_ref, rows)
    height = pairs * 8
    base = nodes - (lanes - 128)
    row_id = iota((height, 128), 0)
    lane_id = iota((height, 128), 1)
    want = jnp.zeros((height, 128), jnp.int32)
    table = []
    for k in range(pairs):
        want = jnp.where(row_id // 8 == k, base + slot_ref[0, k] % 20, want)
        head = rows[k * 16 : (k + 1) * 16, lanes - 128 : lanes].astype(jnp.float32)[0:1]
        table.append(jnp.broadcast_to(head, (8, 128)))
    table = jnp.concatenate(table, axis=0)
    chosen = jnp.sum(jnp.where(lane_id == want, table, 0.0), axis=1, keepdims=True)
    column = (row_id // 8) * 16 + (row_id % 4) * 4 + chosen.astype(jnp.int32)
    hot = (lane_id == column).astype(jnp.float32).astype(jnp.bfloat16)
    hot_ref[...] = hot
    picked = jnp.dot(hot, rows[...], preferred_element_type=jnp.float32)
    fine = jnp.dot(
        picked[:, 0:nodes].astype(jnp.bfloat16),
        up_ref[...],
        preferred_element_type=jnp.float32,
    )
    for k in range(pairs):
        fine_ref[k] = fine[k * 8 : (k + 1) * 8]

    sub_f = iota((8, fine_nodes), 0)

    def prepare(k, src, coefs):
        f = fine_ref[k]
        charge = f[3:4]
        y = f - means[tile_ref[0, k], :, 0:1]
        y_only = jnp.where(sub_f < 3, y, 0.0)
        norm = jnp.sum(y_only * y_only, axis=0, keepdims=True) + REG
        q = jnp.where(sub_f % 4 == 3, norm, -2.0 * y)
        high, mid, low = split3(q)
        first = jnp.where(sub_f < 4, high, mid)
        second = jnp.where(sub_f < 4, low, high)
        third = jnp.where(sub_f < 3, 1.0, 0.0)
        src[...] = jnp.concatenate([first, first, second, third], axis=0).astype(jnp.bfloat16)
        coef = jnp.where(sub_f % 4 == 3, charge, charge * y)
        high, mid, low = split3(coef)
        coefs[...] = jnp.concatenate(
            [jnp.where(sub_f < 4, high, mid), jnp.where(sub_f < 4, low, 0.0)], axis=0
        ).astype(jnp.bfloat16)

    def work(k, src, coefs):
        b = tile_ref[0, k]
        tgt = feats[b]
        total = jnp.zeros((wide, 16), jnp.float32)
        for lo in range(0, fine_nodes, 256):
            hi = min(lo + 256, fine_nodes)
            dist = jnp.dot(tgt, src[:, lo:hi], preferred_element_type=jnp.float32)
            inv = lax.rsqrt(jnp.maximum(dist, REG))
            cube = (inv * inv * inv).astype(jnp.bfloat16)
            cube_ref[k, :, lo:hi] = cube
            total = total + lax.dot_general(
                cube,
                coefs[:, lo:hi],
                (((1,), (1,)), ((), ())),
                preferred_element_type=jnp.float32,
            )
        sums = total.T
        sums = sums[0:8] + sums[8:16]
        sums = sums + jnp.concatenate([sums[4:8], sums[0:4]], axis=0)
        value = (targets[b] * sums[3:4] - sums) * (1.0 / (4.0 * math.pi))
        near[b] += jnp.where(k < count_ref[0, 0], value, 0.0)

    prepare(0, src_a, coef_a)

    def two(i, carry):
        k = 2 * i
        prepare(k + 1, src_b, coef_b)
        work(k, src_a, coef_a)
        prepare(jnp.minimum(k + 2, pairs - 1), src_a, coef_a)
        work(k + 1, src_b, coef_b)
        return carry

    lax.fori_loop(0, pairs // 2, two, 0)

    for copy in copies[3:]:
        copy.wait()
    for d in range(drops):
        for h, (lo, hi) in enumerate(tile_slices(nodes)):
            for c in range(3):
                field[c, d : d + 1, lo:hi] = near[d * 2 + h][c : c + 1, 0:half]
    e = [field[c] + applied_ref[0, c] for c in range(3)]
    n = [normal_ref[c] for c in range(3)]
    along = e[0] * n[0] + e[1] * n[1] + e[2] * n[2]
    square = 0.5 * (e[0] * e[0] + e[1] * e[1] + e[2] * e[2])
    for c in range(3):
        t = along * e[c] - square * n[c]
        trac_ref[c] = t
        block[c * 4 : (c + 1) * 4, 0:nodes] = t * weight_ref[...]
    packed = block[...].astype(jnp.bfloat16)
    for i in range(send_ref.shape[0]):
        send_ref[i] = packed


def stokes_kernel(
    nodes,
    count_ref,
    slot_hbm,
    tile_hbm,
    own_ref,
    side_ref,
    up_ref,
    targets,
    means,
    cube_ref,
    hot_ref,
    fine_ref,
    vel_ref,
    slot_ref,
    tile_ref,
    rows,
    forces,
    flow,
    coef_a,
    coef_b,
    sems,
):
    copies = fetch_all(
        [(slot_hbm, slot_ref), (tile_hbm, tile_ref)], sems
    )
    pairs = slot_ref.shape[1]
    drops = vel_ref.shape[1]
    half = nodes // 2
    fine_nodes = up_ref.shape[1]
    wide = targets.shape[2]
    flow[...] = jnp.zeros_like(flow)
    for copy in copies:
        copy.wait()

    fetch_blocks(slot_ref, own_ref, side_ref, rows)
    picked = jnp.dot(hot_ref[...], rows[...], preferred_element_type=jnp.float32)
    fine = jnp.dot(
        picked[:, 0:nodes].astype(jnp.bfloat16),
        up_ref[...],
        preferred_element_type=jnp.float32,
    )
    for k in range(pairs):
        forces[k] = fine[k * 8 : (k + 1) * 8]

    sub_f = iota((8, fine_nodes), 0)

    def prepare(k, coefs):
        y = fine_ref[k] - means[tile_ref[0, k], :, 0:1]
        f = forces[k]
        y_only = jnp.where(sub_f < 3, y, 0.0)
        norm = jnp.sum(y_only * y_only, axis=0, keepdims=True)
        dot = jnp.sum(y_only * f, axis=0, keepdims=True)
        one = f * jnp.where(sub_f < 4, 1.0, norm)
        two = f * jnp.where(sub_f < 4, y[0:1], y[1:2])
        three = jnp.where(sub_f < 4, f * y[2:3], dot * y)
        parts = [split3(one), split3(two), split3(three)]
        coefs[...] = jnp.concatenate(
            [parts[g][s] for s in range(3) for g in range(3)]
            + [jnp.zeros((8, fine_nodes), jnp.float32)],
            axis=0,
        ).astype(jnp.bfloat16)

    def work(k, coefs):
        b = tile_ref[0, k]
        total = jnp.zeros((wide, 80), jnp.float32)
        for lo in range(0, fine_nodes, 256):
            hi = min(lo + 256, fine_nodes)
            total = total + lax.dot_general(
                cube_ref[k, :, lo:hi],
                coefs[:, lo:hi],
                (((1,), (1,)), ((), ())),
                preferred_element_type=jnp.float32,
            )
        sums = total.T
        sums = sums[0:24] + sums[24:48] + sums[48:72]
        x = targets[b][0:3]
        force, force_sq = sums[0:3], sums[4:7]
        t0, t1, t2 = sums[8:11], sums[12:15], sums[16:19]
        last = sums[20:23]
        x0, x1, x2 = x[0:1], x[1:2], x[2:3]
        square = x0 * x0 + x1 * x1 + x2 * x2
        trace = t0[0:1] + t1[1:2] + t2[2:3]
        reach = jnp.sum(x * force, axis=0, keepdims=True) - trace
        mixed = jnp.concatenate(
            [jnp.sum(x * t, axis=0, keepdims=True) for t in (t0, t1, t2)], axis=0
        )
        v = (square + 2.0 * REG) * force + force_sq
        v = v - 2.0 * (x0 * t0 + x1 * t1 + x2 * t2) + x * reach - mixed + last
        v = v * (1.0 / (8.0 * math.pi))
        flow[b, 0:3, :] += jnp.where(k < count_ref[0, 0], v, 0.0)

    prepare(0, coef_a)

    def two_pairs(i, carry):
        k = 2 * i
        prepare(k + 1, coef_b)
        work(k, coef_a)
        prepare(jnp.minimum(k + 2, pairs - 1), coef_a)
        work(k + 1, coef_b)
        return carry

    lax.fori_loop(0, pairs // 2, two_pairs, 0)
    for d in range(drops):
        for h, (lo, hi) in enumerate(tile_slices(nodes)):
            for c in range(3):
                vel_ref[c, d : d + 1, lo:hi] = flow[d * 2 + h][c : c + 1, 0:half]


def exchange(mine, chips):
    own = lax.all_to_all(mine, ("core", "tgt"), 0, 0)
    moves = [(2 * i, 2 * i + 2) for i in range(chips - 1)]
    moves += [(2 * i + 3, 2 * i + 1) for i in range(chips - 1)]
    side = lax.ppermute(own, ("chip", "core"), moves)
    return own, side


def in_hbm(*arrays):
    return [pltpu.with_memory_space_constraint(a, pltpu.HBM) for a in arrays]


def share(side):
    return lax.all_gather(side, "core")


def local(
    chips,
    positions,
    normals,
    charge,
    weights,
    applied,
    upsample,
    send_list,
    send_count,
    pair_slot,
    pair_tile,
    pair_count,
):
    drops, _, nodes = positions.shape
    fine_nodes = upsample.shape[1]
    pairs = pair_slot.shape[2]
    lanes = ceil_to(nodes + 20, 128)
    wide = ceil_to(nodes // 2, 16)
    tiles = 2 * drops
    f32, bf16 = jnp.float32, jnp.bfloat16
    slots, tile_ids, count = pair_slot[0], pair_tile[0], pair_count

    positions = positions.transpose(1, 0, 2)
    normals = normals.transpose(1, 0, 2)

    i32 = jnp.int32
    dma = pltpu.SemaphoreType.DMA
    mine = pl.pallas_call(
        functools.partial(pack_kernel, nodes),
        out_shape=jax.ShapeDtypeStruct((8, 16, lanes), bf16),
        in_specs=[HBM] * 4,
        out_specs=VMEM,
        scratch_shapes=[
            pltpu.SMEM(send_list.shape[:1:-1], i32),
            pltpu.VMEM((3, drops, nodes), f32),
            pltpu.VMEM((drops, nodes), f32),
            pltpu.VMEM((drops, nodes), f32),
            pltpu.VMEM((16, lanes), f32),
            dma((4,)),
        ],
        compiler_params=pltpu.CompilerParams(vmem_limit_bytes=LIMIT[0]),
        name="pack",
    )(*in_hbm(send_list[0, 0].T, positions, charge, weights))
    own, side = exchange(mine, chips)

    feats, targets, means, up = pl.pallas_call(
        target_kernel,
        out_shape=(
            jax.ShapeDtypeStruct((tiles, wide, 32), bf16),
            jax.ShapeDtypeStruct((tiles, 8, wide), f32),
            jax.ShapeDtypeStruct((tiles, 8, 128), f32),
            jax.ShapeDtypeStruct(upsample.shape, bf16),
        ),
        in_specs=[HBM] * 2,
        out_specs=(VMEM,) * 4,
        scratch_shapes=[pltpu.VMEM((3, drops, nodes), f32), dma((2,))],
        compiler_params=pltpu.CompilerParams(vmem_limit_bytes=LIMIT[0]),
        cost_estimate=pl.CostEstimate(
            flops=4_000_000, bytes_accessed=6_000_000, transcendentals=0
        ),
        name="target",
    )(*in_hbm(positions, upsample))

    traction, forces, cubes, hot, fine = pl.pallas_call(
        functools.partial(field_kernel, nodes),
        out_shape=(
            jax.ShapeDtypeStruct((3, drops, nodes), f32),
            jax.ShapeDtypeStruct((8, 16, lanes), bf16),
            jax.ShapeDtypeStruct((pairs, wide, fine_nodes), bf16),
            jax.ShapeDtypeStruct((pairs * 8, 128), bf16),
            jax.ShapeDtypeStruct((pairs, 8, fine_nodes), f32),
        ),
        in_specs=[SMEM] + [HBM] * 5 + [VMEM] * 6,
        out_specs=(VMEM,) * 5,
        scratch_shapes=[
            pltpu.SMEM((1, pairs), i32),
            pltpu.SMEM((1, pairs), i32),
            pltpu.SMEM((1, 3), f32),
            pltpu.VMEM((3, drops, nodes), f32),
            pltpu.VMEM((drops, nodes), f32),
            pltpu.VMEM((pairs * 16, lanes), bf16),
            pltpu.VMEM((16, lanes), f32),
            pltpu.VMEM((tiles, 8, wide), f32),
            pltpu.VMEM((3, drops, nodes), f32),
            pltpu.VMEM((32, fine_nodes), bf16),
            pltpu.VMEM((32, fine_nodes), bf16),
            pltpu.VMEM((16, fine_nodes), bf16),
            pltpu.VMEM((16, fine_nodes), bf16),
            dma((5,)),
        ],
        compiler_params=pltpu.CompilerParams(vmem_limit_bytes=LIMIT[1]),
        name="field",
    )(
        count, *in_hbm(slots, tile_ids, applied[None], normals, weights),
        own, share(side), up, feats, targets, means,
    )
    own, side = exchange(forces, chips)

    velocity = pl.pallas_call(
        functools.partial(stokes_kernel, nodes),
        out_shape=jax.ShapeDtypeStruct((3, drops, nodes), f32),
        in_specs=[SMEM] + [HBM] * 2 + [VMEM] * 8,
        out_specs=VMEM,
        scratch_shapes=[
            pltpu.SMEM((1, pairs), i32),
            pltpu.SMEM((1, pairs), i32),
            pltpu.VMEM((pairs * 16, lanes), bf16),
            pltpu.VMEM((pairs, 8, fine_nodes), f32),
            pltpu.VMEM((tiles, 8, wide), f32),
            pltpu.VMEM((80, fine_nodes), bf16),
            pltpu.VMEM((80, fine_nodes), bf16),
            dma((2,)),
        ],
        compiler_params=pltpu.CompilerParams(vmem_limit_bytes=LIMIT[2]),
        name="stokes",
    )(count, *in_hbm(slots, tile_ids), own, share(side), up, targets, means, cubes, hot, fine)
    return traction.transpose(1, 0, 2), velocity.transpose(1, 0, 2)


def solution(mesh):
    space, tgt = mesh.shape["space"], mesh.shape["tgt"]
    chips = space // 2
    fine_mesh = Mesh(mesh.devices.reshape(chips, 2, tgt), ("chip", "core", "tgt"))
    every = ("chip", "core", "tgt")
    rows = ("chip", "core")
    placed = (
        P(every, None, None),
        P(every, None, None),
        P(every, None),
        P(every, None),
        P(),
        P(),
        P(rows, "tgt", None, None),
        P(rows, "tgt", None),
        P(rows, "tgt", None),
        P(rows, "tgt", None),
        P(rows, "tgt"),
    )
    return jax.shard_map(
        functools.partial(local, chips),
        mesh=fine_mesh,
        in_specs=placed,
        out_specs=(P(every, None, None), P(every, None, None)),
        check_vma=False,
    )
```

time: 86.7 us -> 62.6 us (0.72)
  Pallas kernels: 31 us -> 19.7 us
  waiting for transfers between devices: 12.2 us -> 2.24 us
  blocking collectives: 20 us -> 28.7 us
  local copies, waits for them, and re-layouts: 8.22 us -> 0 us
  starting transfers between devices: 13.2 us -> 10.2 us
    ppermute x4 -> x2, waiting for transfers between devices: 12.2 us -> 2.24 us  [exchange(): side = lax.ppermute(own, ('chip', 'core'), moves)]
    all_gather x0 -> x2, blocking collectives: none -> 9.48 us  [share(): return lax.all_gather(side, 'core')]
    pallas_call x1, Pallas kernels: 17.1 us -> 10 us  [local(): pl.pallas_call(functools.partial(field_kernel, nodes), out_shape=(jax.Sha...]
    unnamed x16 -> x0, local copies, waits for them, and re-layouts: 6.86 us -> none
    pallas_call x1, Pallas kernels: 12.4 us -> 6.63 us  [local(): pl.pallas_call(functools.partial(stokes_kernel, nodes), out_shape=jax.Sha...]
    ppermute x4 -> x2, starting transfers between devices: 13.2 us -> 10.2 us  [exchange(): side = lax.ppermute(own, ('chip', 'core'), moves)]
    pallas_call x0 -> x1, Pallas kernels: none -> 2.24 us  [local(): pl.pallas_call(target_kernel, out_shape=(jax.ShapeDtypeStruct((tiles, wid...]
    squeeze x1 -> x0, local copies, waits for them, and re-layouts: 1.35 us -> none  [local(): send_list[0, 0]]
  transfers between devices with their start and end apart: 4 -> 2, of which waited for: 3 -> 1; matrix products, arithmetic and copies ran while one was open for 3% -> 0% of each run, Pallas kernels for 0% -> 4%
where the time goes in v2:
time: 62.6 us; the launch traced here: 62.2 us
  blocking collectives  28.7 us (46%)
  Pallas kernels  19.7 us (31%)
  starting transfers between devices  10.2 us (16%)
  waiting for transfers between devices  2.24 us (4%)
  between operations  1.33 us (2%)
    all_to_all x2, blocking collectives, exchange(): own = lax.all_to_all(mine, ('core', 'tgt'), 0, 0)  19.2 us
    ppermute x2, starting transfers between devices, exchange(): side = lax.ppermute(own, ('chip', 'core'), moves)  10.2 us
    pallas_call x1, Pallas kernels, local(): pl.pallas_call(functools.partial(field_kernel, nodes), out_shape=(jax.Sha...  10 us
    all_gather x2, blocking collectives, share(): return lax.all_gather(side, 'core')  9.48 us
    pallas_call x1, Pallas kernels, local(): pl.pallas_call(functools.partial(stokes_kernel, nodes), out_shape=jax.Sha...  6.63 us
    ppermute x2, waiting for transfers between devices, exchange(): side = lax.ppermute(own, ('chip', 'core'), moves)  2.24 us
    pallas_call x1, Pallas kernels, local(): pl.pallas_call(target_kernel, out_shape=(jax.ShapeDtypeStruct((tiles, wid...  2.24 us
  transfers between devices with their start and end apart: 2, of which 1 were waited for; matrix products, arithmetic and copies ran while one was open for 0% of the time, Pallas kernels for 4%

profile of v2, /device:TPU:385, one launch (start us, length us, event | category | flops | bytes accessed | tf_op | source)
XLA Modules:
  0.0 62.2 jit_solution(2314126399565449531)
XLA Ops:
  0.6 0.8 %pack.1 = bf16[8,16,640]{2,1,0:T(8,128)(2,1)S(1)} custom-call(s32[4,5]{1,0:T(4,128)} %bitcast.18, f32[3,4,578]{2,1,0:T(4,128)} %bitcast.14, f32[4,578]{1,0:T(4,128)} %charge_hbm.1, f32[4,578]{1,0:T(4,128)} %weight_hbm.3), custom_call_target="tpu_custom_call" | custom-call | tf_op jit(solution)/shard_map/pack/pallas_call | solution.py:437
  1.5 10.4 %all_to_all.10.own_ref = bf16[8,16,640]{2,1,0:T(8,128)(2,1)S(1)} all-to-all(bf16[8,16,640]{2,1,0:T(8,128)(2,1)S(1)} %pack.1), channel_id=1, replica_groups=mesh['chip'=64,'core'=2,'tgt'=4] {'core','tgt'}, dimensions={0} | all-to-all | bytes 327680 | tf_op jit(solution)/shard_map/all_to_all | solution.py:394
  11.9 6.0 %collective-permute-start = (bf16[8,16,640]{2,1,0:T(8,128)(2,1)S(1)}, bf16[8,16,640]{2,1,0:T(8,128)(2,1)S(1)}, u32[]{:S(2)}, u32[]{:S(2)}) collective-permute-start(bf16[8,16,640]{2,1,0:T(8,128)(2,1)S(1)} %all_to_all.10.own_ref), channel_id=1, source_target_pairs={{0,8},{8,16},{16,24},{24,32},{32,40},{40,48},{48,56},{56,64},{64,7... | collective-permute-start | bytes 491528 | tf_op jit(solution)/shard_map/ppermute | solution.py:397
  18.6 2.2 %target.1 = (bf16[8,304,32]{2,1,0:T(8,128)(2,1)S(1)}, f32[8,8,304]{2,1,0:T(8,128)S(1)}, f32[8,8,128]{2,1,0:T(8,128)S(1)}, bf16[578,2112]{1,0:T(8,128)(2,1)S(1)}) custom-call(f32[3,4,578]{2,1,0:T(4,128)} %bitcast.15, bf16[578,2112]{1,0:T(8,128)(2,1)} %up_hbm.1), custom_call_target="tpu_custom_call" | custom-call | flops 4000000 | bytes 6000000 | tf_op jit(solution)/shard_map/target/pallas_call | solution.py:455
  20.8 0.0 collective-permute-done
  20.8 3.5 %all-gather = bf16[16,16,640]{2,1,0:T(8,128)(2,1)S(1)} all-gather(bf16[8,16,640]{2,1,0:T(8,128)(2,1)S(1)} %collective-permute-done), channel_id=2, replica_groups=mesh['chip'=64,'core'=2,'tgt'=4] {'core'}, dimensions={0}, use_global_device_ids=true | all-gather | bytes 491520 | tf_op jit(solution)/shard_map/all_gather | solution.py:406
  24.3 10.0 %field.1 = (f32[3,4,578]{2,1,0:T(4,128)}, bf16[8,16,640]{2,1,0:T(8,128)(2,1)S(1)}, bf16[8,304,2112]{2,1,0:T(8,128)(2,1)S(1)}, bf16[64,128]{1,0:T(8,128)(2,1)S(1)}, f32[8,8,2112]{2,1,0:T(8,128)S(1)}) custom-call(s32[1,1]{1,0:T(1,128)S(6)} %copy.12.count_ref, s32[1,8]{1,0:T(1,128)} %bitcast.19, s32[1,8]{1,0:T(1,128)} %bitcast.21, f32[1,3]{1,0:T(1,128)} %bitcast.23, ...), custom_call_target="tpu_custom_call" | custom-call | tf_op jit(solution)/shard_map/field/pallas_call | solution.py:473
  34.3 8.8 %all_to_all.11.own_ref = bf16[8,16,640]{2,1,0:T(8,128)(2,1)S(1)} all-to-all(bf16[8,16,640]{2,1,0:T(8,128)(2,1)S(1)} %get-tuple-element.16), channel_id=1, replica_groups=mesh['chip'=64,'core'=2,'tgt'=4] {'core','tgt'}, dimensions={0} | all-to-all | bytes 327680 | tf_op jit(solution)/shard_map/all_to_all | solution.py:394
  43.2 4.2 %collective-permute-start.1 = (bf16[8,16,640]{2,1,0:T(8,128)(2,1)S(1)}, bf16[8,16,640]{2,1,0:T(8,128)(2,1)S(1)}, u32[]{:S(2)}, u32[]{:S(2)}) collective-permute-start(bf16[8,16,640]{2,1,0:T(8,128)(2,1)S(1)} %all_to_all.11.own_ref), channel_id=1, source_target_pairs={{0,8},{8,16},{16,24},{24,32},{32,40},{40,48},{48,56},{56,64},{64,7... | collective-permute-start | bytes 491528 | tf_op jit(solution)/shard_map/ppermute | solution.py:397
  47.4 2.2 %collective-permute-done.1 = bf16[8,16,640]{2,1,0:T(8,128)(2,1)S(1)} collective-permute-done((bf16[8,16,640]{2,1,0:T(8,128)(2,1)S(1)}, bf16[8,16,640]{2,1,0:T(8,128)(2,1)S(1)}, u32[]{:S(2)}, u32[]{:S(2)}) %collective-permute-start.1) | collective-permute-done | bytes 163872 | tf_op jit(solution)/shard_map/ppermute | solution.py:397
  49.6 6.0 %all-gather.1 = bf16[16,16,640]{2,1,0:T(8,128)(2,1)S(1)} all-gather(bf16[8,16,640]{2,1,0:T(8,128)(2,1)S(1)} %collective-permute-done.1), channel_id=3, replica_groups=mesh['chip'=64,'core'=2,'tgt'=4] {'core'}, dimensions={0}, use_global_device_ids=true | all-gather | bytes 491520 | tf_op jit(solution)/shard_map/all_gather | solution.py:406
  55.6 6.6 %stokes.1 = f32[3,4,578]{2,1,0:T(4,128)} custom-call(s32[1,1]{1,0:T(1,128)S(6)} %copy.12.count_ref, s32[1,8]{1,0:T(1,128)} %bitcast.20, s32[1,8]{1,0:T(1,128)} %bitcast.22, bf16[8,16,640]{2,1,0:T(8,128)(2,1)S(1)} %all_to_all.11.own_ref, bf16[2,8,16,640]{3,2,1,0:T(8,128)(2,1)S(1)} %bitcast.13, bf16[578,2112]{1,0:T(8,128)(2,1)S(1)} %get-tuple-element.11.up_ref, ...), custom_call_target="tpu_custom_call" | custom-call | tf_op jit(solution)/shard_map/stokes/pallas_call | solution.py:508
Async XLA Ops:
  11.9 8.9 %collective-permute-start = (bf16[8,16,640]{2,1,0:T(8,128)(2,1)S(1)}, bf16[8,16,640]{2,1,0:T(8,128)(2,1)S(1)}, u32[]{:S(2)}, u32[]{:S(2)}) collective-permute-start(bf16[8,16,640]{2,1,0:T(8,128)(2,1)S(1)} %all_to_all.10.own_ref), channel_id=1, source_target_pairs={{0,8},{8,16},{16,24},{24,32},{32,40},{40,48},{48,56},{56,64},{64,7... | collective-permute-start | bytes 491528 | tf_op jit(solution)/shard_map/ppermute | solution.py:397
  43.2 6.4 %collective-permute-start.1 = (bf16[8,16,640]{2,1,0:T(8,128)(2,1)S(1)}, bf16[8,16,640]{2,1,0:T(8,128)(2,1)S(1)}, u32[]{:S(2)}, u32[]{:S(2)}) collective-permute-start(bf16[8,16,640]{2,1,0:T(8,128)(2,1)S(1)} %all_to_all.11.own_ref), channel_id=1, source_target_pairs={{0,8},{8,16},{16,24},{24,32},{32,40},{40,48},{48,56},{56,64},{64,7... | collective-permute-start | bytes 491528 | tf_op jit(solution)/shard_map/ppermute | solution.py:397

commit v3 on v2

v3 whole, which is shorter than its diff:
```python
import functools
import math

import jax
import jax.numpy as jnp
from jax import lax
from jax.experimental import pallas as pl
from jax.experimental.pallas import tpu as pltpu
from jax.sharding import Mesh
from jax.sharding import PartitionSpec as P

REG = 0.25
VMEM = pl.BlockSpec(memory_space=pltpu.VMEM)
HBM = pl.BlockSpec(memory_space=pltpu.HBM)
SMEM = pl.BlockSpec(memory_space=pltpu.SMEM)
VECTOR_CHUNKS = (2, 5, 8)
LIMIT = (2 << 20, 20 << 20, 20 << 20)


def ceil_to(n, m):
    return -(-n // m) * m


def iota(shape, dim):
    return lax.broadcasted_iota(jnp.int32, shape, dim)


def split3(x):
    high = x.astype(jnp.bfloat16).astype(jnp.float32)
    rest = x - high
    mid = rest.astype(jnp.bfloat16).astype(jnp.float32)
    low = (rest - mid).astype(jnp.bfloat16).astype(jnp.float32)
    return high, mid, low


def fetch_all(pairs, sems):
    copies = [
        pltpu.make_async_copy(src, dst, sems.at[i]) for i, (src, dst) in enumerate(pairs)
    ]
    for copy in copies:
        copy.start()
    return copies


def pack_kernel(
    nodes, send_hbm, pos_hbm, charge_hbm, weight_hbm, out_ref,
    send_ref, pos_ref, charge_ref, weight_ref, block, sems,
):
    copies = fetch_all(
        [
            (send_hbm, send_ref),
            (pos_hbm, pos_ref),
            (charge_hbm, charge_ref),
            (weight_hbm, weight_ref),
        ],
        sems,
    )
    lanes = block.shape[1]
    block[...] = jnp.zeros_like(block)
    for copy in copies:
        copy.wait()
    for c in range(3):
        block[c * 4 : (c + 1) * 4, 0:nodes] = pos_ref[c]
    block[12:16, 0:nodes] = charge_ref[...] * weight_ref[...]
    base = nodes - (lanes - 128)
    lane = iota((1, 128), 1)
    row = block[0:1, lanes - 128 : lanes]
    slots, shell = send_ref.shape
    for o in range(shell):
        for j in range(slots):
            row = jnp.where(
                lane == base + o * slots + j, send_ref[j, o].astype(jnp.float32), row
            )
    block[0:1, lanes - 128 : lanes] = row
    packed = block[...].astype(jnp.bfloat16)
    for i in range(out_ref.shape[0]):
        out_ref[i] = packed


def block_index(p, core):
    place = core + 4 - (p // 4) % 5
    return ((place // 2) * 8 + (place % 2) * 4 + p // 20) * 16


def select(hot, own_ref, side_ref, lo):
    total = None
    for i, ref in enumerate((side_ref.at[0], own_ref, side_ref.at[1])):
        blocks = ref[...]
        blocks = blocks.reshape(blocks.shape[0] * blocks.shape[1], blocks.shape[2])
        part = jnp.dot(
            hot[:, i * 128 : (i + 1) * 128],
            blocks[:, lo:],
            preferred_element_type=jnp.float32,
        )
        total = part if total is None else total + part
    return total


def inverse_cube(d):
    d = jnp.maximum(d.astype(jnp.bfloat16), jnp.bfloat16(REG))
    return lax.rsqrt(d * d * d)


def tile_slices(nodes):
    half = nodes // 2
    return [(0, half), (half, nodes)]


def target_kernel(
    count_ref, pos_hbm, slot_hbm, tile_hbm, applied_hbm, up_hbm, normal_hbm, weight_hbm,
    feat_ref, target_ref, mean_ref, wide_ref, head_ref, base_ref, want_ref, mask_ref,
    applied_ref, up_ref, normal_ref, weight_ref,
    pos_ref, slot_ref, tile_ref, ambient_ref, tiles, means, sems,
):
    copies = fetch_all(
        [
            (pos_hbm, pos_ref),
            (slot_hbm, slot_ref),
            (tile_hbm, tile_ref),
            (applied_hbm, ambient_ref),
            (up_hbm, up_ref),
            (normal_hbm, normal_ref),
            (weight_hbm, weight_ref),
        ],
        sems,
    )
    for copy in copies[:4]:
        copy.wait()
    core = lax.axis_index("core")
    pairs = slot_ref.shape[1]
    drops, nodes = pos_ref.shape[1:]
    half = nodes // 2
    wide = feat_ref.shape[1]

    height = head_ref.shape[0]
    row = iota((height, 128), 0)
    start = jnp.zeros((height, 128), jnp.int32)
    want = jnp.zeros((height, 128), jnp.int32)
    for k in range(pairs):
        p = slot_ref[0, k]
        start = jnp.where(row // 8 == k, block_index(p, core), start)
        want = jnp.where(row // 8 == k, nodes % 128 + p % 20, want)
    lane = iota((height, 128), 1)
    base_ref[...] = start + (row % 4) * 4
    want_ref[...] = want
    for i in range(3):
        head = (lane + i * 128 == start).astype(jnp.float32)
        head_ref[:, i * 128 : (i + 1) * 128] = head.astype(jnp.bfloat16)

    for c in range(3):
        applied_ref[c] = jnp.full(applied_ref.shape[1:], ambient_ref[0, c], jnp.float32)
    pair_id = iota((pairs, wide), 0)
    owner = jnp.full((pairs, wide), -1, jnp.int32)
    for k in range(pairs):
        mine = jnp.where(k < count_ref[0, 0], tile_ref[0, k], -1)
        owner = jnp.where(pair_id == k, mine, owner)
    for b in range(2 * drops):
        mask_ref[b] = (owner == b).astype(jnp.float32)

    tiles[...] = jnp.zeros_like(tiles)
    means[...] = jnp.zeros_like(means)
    for d in range(drops):
        for h, (lo, hi) in enumerate(tile_slices(nodes)):
            for c in range(3):
                line = pos_ref[c, d : d + 1, lo:hi]
                mean = jnp.sum(line, axis=1, keepdims=True) / half
                tiles[d * 2 + h, c : c + 1, 0:half] = line - mean
                means[d * 2 + h, c : c + 1, :] = jnp.broadcast_to(mean, (1, 128))
                means[d * 2 + h, c + 4 : c + 5, :] = jnp.broadcast_to(mean, (1, 128))
    sub = iota((8, wide), 0)
    part = iota((32, 512), 0)
    comp = iota((32, 512), 1) // 128
    coord = (part == comp) | (part == 8 + comp) | (part == 20 + comp)
    length = (part >= 24) & (part < 27)
    pick = ((comp < 3) & coord) | ((comp == 3) & length)
    pick = pick.astype(jnp.float32).astype(jnp.bfloat16)
    for k in range(pairs):
        b = tile_ref[0, k]
        t = tiles[b]
        target_ref[k] = t
        mean_ref[k] = means[b]
        norm = jnp.sum(t * t, axis=0, keepdims=True)
        t8 = jnp.where(sub < 4, t, jnp.concatenate([t[4:8], t[0:4]], axis=0))
        t8 = jnp.where(sub % 4 == 3, 1.0, t8)
        high, mid, low = split3(t8)
        nh, nm, nl = split3(norm)
        last = jnp.where(
            sub == 0, nh, jnp.where(sub == 1, nm, jnp.where(sub == 2, nl, 0.0))
        )
        stack = jnp.concatenate([high, mid, jnp.where(sub < 4, high, low), last], axis=0)
        feat_ref[k] = stack.T.astype(jnp.bfloat16)
        spread = jnp.dot(feat_ref[k], pick, preferred_element_type=jnp.float32)
        for c in range(4):
            wide_ref[k, c] = spread[:, c * 128 : (c + 1) * 128]
    for copy in copies[4:]:
        copy.wait()


def gather_tiles(values, mask_ref, b, rows):
    total = None
    for k in range(values.shape[0]):
        live = mask_ref[b, k : k + 1, :] > 0.5
        part = jnp.where(live, values[k, 0:rows, :], 0.0)
        total = part if total is None else total + part
    return total


def field_kernel(
    nodes,
    own_ref,
    side_ref,
    feats,
    targets,
    means,
    lanes_x,
    head_ref,
    base_ref,
    want_ref,
    mask_ref,
    applied_ref,
    up_ref,
    normal_ref,
    weight_ref,
    trac_ref,
    send_ref,
    cube_ref,
    hot_ref,
    fine_ref,
    block,
    values,
    field,
    src_a,
    src_b,
    coef_a,
    coef_b,
    row_a,
    row_b,
):
    pairs = values.shape[0]
    drops = weight_ref.shape[0]
    half = nodes // 2
    wide = feats.shape[1]
    fine_nodes = up_ref.shape[1]

    height = pairs * 8
    lane_id = iota((height, 128), 1)
    table = select(head_ref[...], own_ref, side_ref, nodes // 128 * 128)
    chosen = jnp.sum(
        jnp.where(lane_id == want_ref[...], table, 0.0), axis=1, keepdims=True
    )
    column = base_ref[...] + chosen.astype(jnp.int32)
    for i in range(3):
        hot = (lane_id + i * 128 == column).astype(jnp.float32)
        hot_ref[:, i * 128 : (i + 1) * 128] = hot.astype(jnp.bfloat16)
    picked = select(hot_ref[...], own_ref, side_ref, 0)
    fine = jnp.dot(
        picked[:, 0:nodes].astype(jnp.bfloat16),
        up_ref[...],
        preferred_element_type=jnp.float32,
    )
    for k in range(pairs):
        fine_ref[k] = fine[k * 8 : (k + 1) * 8]

    sub_f = iota((8, fine_nodes), 0)

    def prepare(k, src, coefs, qrow):
        f = fine_ref[k]
        charge = f[3:4]
        y = f - means[k, :, 0:1]
        y_only = jnp.where(sub_f < 3, y, 0.0)
        norm = jnp.sum(y_only * y_only, axis=0, keepdims=True) + REG
        q = jnp.where(sub_f % 4 == 3, norm, -2.0 * y)
        qrow[...] = q
        high, mid, low = split3(q)
        first = jnp.where(sub_f < 4, high, mid)
        second = jnp.where(sub_f < 4, low, high)
        third = jnp.where(sub_f < 3, 1.0, 0.0)
        src[...] = jnp.concatenate([first, first, second, third], axis=0).astype(jnp.bfloat16)
        coef = jnp.where(sub_f % 4 == 3, charge, charge * y)
        high, mid, low = split3(coef)
        coefs[...] = jnp.concatenate(
            [jnp.where(sub_f < 4, high, mid), jnp.where(sub_f < 4, low, 0.0)], axis=0
        ).astype(jnp.bfloat16)

    def work(k, src, coefs, qrow):
        tgt = feats[k]
        total = jnp.zeros((wide, 16), jnp.float32)
        for lo in range(0, fine_nodes, 256):
            hi = min(lo + 256, fine_nodes)
            if lo // 256 in VECTOR_CHUNKS:
                parts = []
                for at in range(lo, hi, 128):
                    end = min(at + 128, hi)
                    d = lanes_x[k, 3][:, : end - at] + qrow[3:4, at:end]
                    for c in range(3):
                        d = d + lanes_x[k, c][:, : end - at] * qrow[c : c + 1, at:end]
                    parts.append(inverse_cube(d))
                cube = jnp.concatenate(parts, axis=1) if len(parts) > 1 else parts[0]
            else:
                dist = jnp.dot(tgt, src[:, lo:hi], preferred_element_type=jnp.float32)
                cube = inverse_cube(dist)
            cube_ref[k, :, lo:hi] = cube
            total = total + lax.dot_general(
                cube,
                coefs[:, lo:hi],
                (((1,), (1,)), ((), ())),
                preferred_element_type=jnp.float32,
            )
        sums = total.T
        sums = sums[0:8] + sums[8:16]
        sums = sums + jnp.concatenate([sums[4:8], sums[0:4]], axis=0)
        values[k] = (targets[k] * sums[3:4] - sums) * (1.0 / (4.0 * math.pi))

    prepare(0, src_a, coef_a, row_a)

    def two(i, carry):
        k = 2 * i
        prepare(k + 1, src_b, coef_b, row_b)
        work(k, src_a, coef_a, row_a)
        prepare(jnp.minimum(k + 2, pairs - 1), src_a, coef_a, row_a)
        work(k + 1, src_b, coef_b, row_b)
        return carry

    lax.fori_loop(0, pairs // 2, two, 0)

    block[...] = jnp.zeros_like(block)
    for d in range(drops):
        for h, (lo, hi) in enumerate(tile_slices(nodes)):
            near = gather_tiles(values, mask_ref, d * 2 + h, 8)
            for c in range(3):
                field[c, d : d + 1, lo:hi] = near[c : c + 1, 0:half]
    e = [field[c] + applied_ref[c, :, 0:nodes] for c in range(3)]
    n = [normal_ref[c] for c in range(3)]
    along = e[0] * n[0] + e[1] * n[1] + e[2] * n[2]
    square = 0.5 * (e[0] * e[0] + e[1] * e[1] + e[2] * e[2])
    for c in range(3):
        t = along * e[c] - square * n[c]
        trac_ref[c] = t
        block[c * 4 : (c + 1) * 4, 0:nodes] = t * weight_ref[...]
    packed = block[...].astype(jnp.bfloat16)
    for i in range(send_ref.shape[0]):
        send_ref[i] = packed


def stokes_kernel(
    nodes,
    own_ref,
    side_ref,
    targets,
    means,
    mask_ref,
    up_ref,
    cube_ref,
    hot_ref,
    fine_ref,
    trac_ref,
    vel_ref,
    trac_hbm,
    forces,
    values,
    coef_a,
    coef_b,
    sems,
):
    copies = fetch_all([(trac_ref, trac_hbm)], sems)
    pairs = values.shape[0]
    drops = vel_ref.shape[1]
    half = nodes // 2
    fine_nodes = up_ref.shape[1]
    wide = targets.shape[2]

    picked = select(hot_ref[...], own_ref, side_ref, 0)
    fine = jnp.dot(
        picked[:, 0:nodes].astype(jnp.bfloat16),
        up_ref[...],
        preferred_element_type=jnp.float32,
    )
    for k in range(pairs):
        forces[k] = fine[k * 8 : (k + 1) * 8]

    sub_f = iota((8, fine_nodes), 0)

    def prepare(k, coefs):
        y = fine_ref[k] - means[k, :, 0:1]
        f = forces[k]
        y_only = jnp.where(sub_f < 3, y, 0.0)
        norm = jnp.sum(y_only * y_only, axis=0, keepdims=True)
        dot = jnp.sum(y_only * f, axis=0, keepdims=True)
        one = f * jnp.where(sub_f < 4, 1.0, norm)
        two = f * jnp.where(sub_f < 4, y[0:1], y[1:2])
        three = jnp.where(sub_f < 4, f * y[2:3], dot * y)
        parts = [split3(one), split3(two), split3(three)]
        coefs[...] = jnp.concatenate(
            [parts[g][s] for s in range(3) for g in range(3)]
            + [jnp.zeros((8, fine_nodes), jnp.float32)],
            axis=0,
        ).astype(jnp.bfloat16)

    def work(k, coefs):
        total = jnp.zeros((wide, 80), jnp.float32)
        for lo in range(0, fine_nodes, 256):
            hi = min(lo + 256, fine_nodes)
            total = total + lax.dot_general(
                cube_ref[k, :, lo:hi],
                coefs[:, lo:hi],
                (((1,), (1,)), ((), ())),
                preferred_element_type=jnp.float32,
            )
        sums = total.T
        sums = sums[0:24] + sums[24:48] + sums[48:72]
        x = targets[k][0:3]
        force, force_sq = sums[0:3], sums[4:7]
        t0, t1, t2 = sums[8:11], sums[12:15], sums[16:19]
        last = sums[20:23]
        x0, x1, x2 = x[0:1], x[1:2], x[2:3]
        square = x0 * x0 + x1 * x1 + x2 * x2
        trace = t0[0:1] + t1[1:2] + t2[2:3]
        reach = jnp.sum(x * force, axis=0, keepdims=True) - trace
        mixed = jnp.concatenate(
            [jnp.sum(x * t, axis=0, keepdims=True) for t in (t0, t1, t2)], axis=0
        )
        v = (square + 2.0 * REG) * force + force_sq
        v = v - 2.0 * (x0 * t0 + x1 * t1 + x2 * t2) + x * reach - mixed + last
        values[k, 0:3, :] = v * (1.0 / (8.0 * math.pi))

    prepare(0, coef_a)

    def two_pairs(i, carry):
        k = 2 * i
        prepare(k + 1, coef_b)
        work(k, coef_a)
        prepare(jnp.minimum(k + 2, pairs - 1), coef_a)
        work(k + 1, coef_b)
        return carry

    lax.fori_loop(0, pairs // 2, two_pairs, 0)
    for d in range(drops):
        for h, (lo, hi) in enumerate(tile_slices(nodes)):
            flow = gather_tiles(values, mask_ref, d * 2 + h, 3)
            for c in range(3):
                vel_ref[c, d : d + 1, lo:hi] = flow[c : c + 1, 0:half]
    copies[0].wait()


def exchange(mine, chips):
    own = lax.all_to_all(mine, ("core", "tgt"), 0, 0)
    moves = [(2 * i, 2 * i + 2) for i in range(chips - 1)]
    moves += [(2 * i + 3, 2 * i + 1) for i in range(chips - 1)]
    side = lax.ppermute(own, ("chip", "core"), moves)
    return own, side


def in_hbm(*arrays):
    return [pltpu.with_memory_space_constraint(a, pltpu.HBM) for a in arrays]


def share(side):
    return lax.all_gather(side, "core")


def local(
    chips,
    positions,
    normals,
    charge,
    weights,
    applied,
    upsample,
    send_list,
    send_count,
    pair_slot,
    pair_tile,
    pair_count,
):
    drops, _, nodes = positions.shape
    fine_nodes = upsample.shape[1]
    pairs = pair_slot.shape[2]
    lanes = ceil_to(nodes + 20, 128)
    wide = ceil_to(nodes // 2, 16)
    tiles = 2 * drops
    f32, bf16 = jnp.float32, jnp.bfloat16
    slots, tile_ids, count = pair_slot[0], pair_tile[0], pair_count

    positions = positions.transpose(1, 0, 2)
    normals = normals.transpose(1, 0, 2)

    i32 = jnp.int32
    dma = pltpu.SemaphoreType.DMA
    mine = pl.pallas_call(
        functools.partial(pack_kernel, nodes),
        out_shape=jax.ShapeDtypeStruct((8, 16, lanes), bf16),
        in_specs=[HBM] * 4,
        out_specs=VMEM,
        scratch_shapes=[
            pltpu.SMEM(send_list.shape[:1:-1], i32),
            pltpu.VMEM((3, drops, nodes), f32),
            pltpu.VMEM((drops, nodes), f32),
            pltpu.VMEM((drops, nodes), f32),
            pltpu.VMEM((16, lanes), f32),
            dma((4,)),
        ],
        compiler_params=pltpu.CompilerParams(vmem_limit_bytes=LIMIT[0]),
        name="pack",
    )(*in_hbm(send_list[0, 0].T, positions, charge, weights))
    own, side = exchange(mine, chips)

    shape = jax.ShapeDtypeStruct
    info = pl.pallas_call(
        target_kernel,
        out_shape=(
            shape((pairs, wide, 32), bf16),
            shape((pairs, 8, wide), f32),
            shape((pairs, 8, 128), f32),
            shape((pairs, 4, wide, 128), f32),
            shape((pairs * 8, 384), bf16),
            shape((pairs * 8, 128), i32),
            shape((pairs * 8, 128), i32),
            shape((tiles, pairs, wide), f32),
            shape((3, drops, lanes), f32),
            shape(upsample.shape, bf16),
            shape((3, drops, nodes), f32),
            shape((drops, nodes), f32),
        ),
        in_specs=[SMEM] + [HBM] * 7,
        out_specs=(VMEM,) * 12,
        scratch_shapes=[
            pltpu.VMEM((3, drops, nodes), f32),
            pltpu.SMEM((1, pairs), i32),
            pltpu.SMEM((1, pairs), i32),
            pltpu.SMEM((1, 3), f32),
            pltpu.VMEM((tiles, 8, wide), f32),
            pltpu.VMEM((tiles, 8, 128), f32),
            dma((7,)),
        ],
        compiler_params=pltpu.CompilerParams(vmem_limit_bytes=LIMIT[0]),
        cost_estimate=pl.CostEstimate(
            flops=4_000_000, bytes_accessed=6_000_000, transcendentals=0
        ),
        name="target",
    )(count, *in_hbm(positions, slots, tile_ids, applied[None], upsample, normals, weights))
    targets, means, mask, up = info[1], info[2], info[7], info[9]

    traction, forces, cubes, hot, fine = pl.pallas_call(
        functools.partial(field_kernel, nodes),
        out_shape=(
            shape((3, drops, nodes), f32),
            shape((8, 16, lanes), bf16),
            shape((pairs, wide, fine_nodes), bf16),
            shape((pairs * 8, 384), bf16),
            shape((pairs, 8, fine_nodes), f32),
        ),
        in_specs=[VMEM] * 14,
        out_specs=(VMEM,) * 5,
        scratch_shapes=[
            pltpu.VMEM((16, lanes), f32),
            pltpu.VMEM((pairs, 8, wide), f32),
            pltpu.VMEM((3, drops, nodes), f32),
            pltpu.VMEM((32, fine_nodes), bf16),
            pltpu.VMEM((32, fine_nodes), bf16),
            pltpu.VMEM((16, fine_nodes), bf16),
            pltpu.VMEM((16, fine_nodes), bf16),
            pltpu.VMEM((8, fine_nodes), f32),
            pltpu.VMEM((8, fine_nodes), f32),
        ],
        compiler_params=pltpu.CompilerParams(vmem_limit_bytes=LIMIT[1]),
        name="field",
    )(own, share(side), *info)
    own, side = exchange(forces, chips)

    velocity, traction = pl.pallas_call(
        functools.partial(stokes_kernel, nodes),
        out_shape=(shape((3, drops, nodes), f32),) * 2,
        in_specs=[VMEM] * 10,
        out_specs=(VMEM, HBM),
        scratch_shapes=[
            pltpu.VMEM((pairs, 8, fine_nodes), f32),
            pltpu.VMEM((pairs, 8, wide), f32),
            pltpu.VMEM((80, fine_nodes), bf16),
            pltpu.VMEM((80, fine_nodes), bf16),
            dma((1,)),
        ],
        compiler_params=pltpu.CompilerParams(vmem_limit_bytes=LIMIT[2]),
        name="stokes",
    )(own, share(side), targets, means, mask, up, cubes, hot, fine, traction)
    return traction.transpose(1, 0, 2), velocity.transpose(1, 0, 2)


def solution(mesh):
    space, tgt = mesh.shape["space"], mesh.shape["tgt"]
    chips = space // 2
    fine_mesh = Mesh(mesh.devices.reshape(chips, 2, tgt), ("chip", "core", "tgt"))
    every = ("chip", "core", "tgt")
    rows = ("chip", "core")
    placed = (
        P(every, None, None),
        P(every, None, None),
        P(every, None),
        P(every, None),
        P(),
        P(),
        P(rows, "tgt", None, None),
        P(rows, "tgt", None),
        P(rows, "tgt", None),
        P(rows, "tgt", None),
        P(rows, "tgt"),
    )
    return jax.shard_map(
        functools.partial(local, chips),
        mesh=fine_mesh,
        in_specs=placed,
        out_specs=(P(every, None, None), P(every, None, None)),
        check_vma=False,
    )
```

time: 62.6 us -> 60.1 us (0.960)
  Pallas kernels: 19.7 us -> 17.1 us
    pallas_call x3, Pallas kernels: 18.9 us -> 16.3 us  [the longest x1 8.46 us: local(): pl.pallas_call(functools.partial(field_kernel, nodes), out_shape=(shape((...]
  transfers between devices with their start and end apart: 2 -> 2, of which waited for: 1 -> 1; matrix products, arithmetic and copies ran while one was open for 0% -> 0% of each run, Pallas kernels for 4% -> 3%
where the time goes in v3:
time: 60.1 us; the launch traced here: 59.8 us
  blocking collectives  28.9 us (48%)
  Pallas kernels  17.1 us (28%)
  starting transfers between devices  10.2 us (17%)
  waiting for transfers between devices  2.24 us (4%)
  between operations  1.33 us (2%)
    all_to_all x2, blocking collectives, exchange(): own = lax.all_to_all(mine, ('core', 'tgt'), 0, 0)  19.2 us
    ppermute x2, starting transfers between devices, exchange(): side = lax.ppermute(own, ('chip', 'core'), moves)  10.2 us
    all_gather x2, blocking collectives, share(): return lax.all_gather(side, 'core')  9.68 us
    pallas_call x1, Pallas kernels, local(): pl.pallas_call(functools.partial(field_kernel, nodes), out_shape=(shape((...  8.46 us
    pallas_call x1, Pallas kernels, local(): pl.pallas_call(functools.partial(stokes_kernel, nodes), out_shape=(shape(...  5.76 us
    ppermute x2, waiting for transfers between devices, exchange(): side = lax.ppermute(own, ('chip', 'core'), moves)  2.24 us
    pallas_call x1, Pallas kernels, local(): pl.pallas_call(target_kernel, out_shape=(shape((pairs, wide, 32), bf16),...  2.05 us
  transfers between devices with their start and end apart: 2, of which 1 were waited for; matrix products, arithmetic and copies ran while one was open for 0% of the time, Pallas kernels for 3%

profile of v3, /device:TPU:385, one launch (start us, length us, event | category | flops | bytes accessed | tf_op | source)
XLA Modules:
  0.0 59.8 jit_solution(11732187310402804675)
XLA Ops:
  0.6 0.8 %pack.1 = bf16[8,16,640]{2,1,0:T(8,128)(2,1)S(1)} custom-call(s32[4,5]{1,0:T(4,128)} %bitcast.17, f32[3,4,578]{2,1,0:T(4,128)} %bitcast.14, f32[4,578]{1,0:T(4,128)} %charge_hbm.1, f32[4,578]{1,0:T(4,128)} %weight_hbm.3), custom_call_target="tpu_custom_call" | custom-call | tf_op jit(solution)/shard_map/pack/pallas_call | solution.py:489
  1.5 10.4 %all_to_all.10.own_ref = bf16[8,16,640]{2,1,0:T(8,128)(2,1)S(1)} all-to-all(bf16[8,16,640]{2,1,0:T(8,128)(2,1)S(1)} %pack.1), channel_id=1, replica_groups=mesh['chip'=64,'core'=2,'tgt'=4] {'core','tgt'}, dimensions={0} | all-to-all | bytes 327680 | tf_op jit(solution)/shard_map/all_to_all | solution.py:446
  11.9 6.0 %collective-permute-start = (bf16[8,16,640]{2,1,0:T(8,128)(2,1)S(1)}, bf16[8,16,640]{2,1,0:T(8,128)(2,1)S(1)}, u32[]{:S(2)}, u32[]{:S(2)}) collective-permute-start(bf16[8,16,640]{2,1,0:T(8,128)(2,1)S(1)} %all_to_all.10.own_ref), channel_id=1, source_target_pairs={{0,8},{8,16},{16,24},{24,32},{32,40},{40,48},{48,56},{56,64},{64,7... | collective-permute-start | bytes 491528 | tf_op jit(solution)/shard_map/ppermute | solution.py:449
  18.6 2.0 %target.1 = (bf16[8,304,32]{2,1,0:T(8,128)(2,1)S(1)}, f32[8,8,304]{2,1,0:T(8,128)S(1)}, f32[8,8,128]{2,1,0:T(8,128)S(1)}, f32[8,4,304,128]{3,2,1,0:T(8,128)S(1)}...) custom-call(s32[1,1]{1,0:T(1,128)S(6)} %copy.12.count_ref, ...), custom_call_target="tpu_custom_call" | custom-call | flops 4000000 | bytes 6000000 | tf_op jit(solution)/shard_map/target/pallas_call | solution.py:508
  20.6 0.0 collective-permute-done
  20.6 3.7 %all-gather = bf16[16,16,640]{2,1,0:T(8,128)(2,1)S(1)} all-gather(bf16[8,16,640]{2,1,0:T(8,128)(2,1)S(1)} %collective-permute-done), channel_id=2, replica_groups=mesh['chip'=64,'core'=2,'tgt'=4] {'core'}, dimensions={0}, use_global_device_ids=true | all-gather | bytes 491520 | tf_op jit(solution)/shard_map/all_gather | solution.py:458
  24.3 8.5 %field.1 = (f32[3,4,578]{2,1,0:T(4,128)S(1)}, bf16[8,16,640]{2,1,0:T(8,128)(2,1)S(1)}, bf16[8,304,2112]{2,1,0:T(8,128)(2,1)S(1)}, bf16[64,384]{1,0:T(8,128)(2,1)S(1)}, f32[8,8,2112]{2,1,0:T(8,128)S(1)}) custom-call(bf16[8,16,640]{2,1,0:T(8,128)(2,1)S(1)} %all_to_all.10.own_ref, bf16[2,8,16,640]{3,2,1,0:T(8,128)(2,1)S(1)} %bitcast.12, ...), custom_call_target="tpu_custom_call" | custom-call | tf_op jit(solution)/shard_map/field/pallas_call | solution.py:543
  32.8 8.8 %all_to_all.11.own_ref = bf16[8,16,640]{2,1,0:T(8,128)(2,1)S(1)} all-to-all(bf16[8,16,640]{2,1,0:T(8,128)(2,1)S(1)} %get-tuple-element.33), channel_id=1, replica_groups=mesh['chip'=64,'core'=2,'tgt'=4] {'core','tgt'}, dimensions={0} | all-to-all | bytes 327680 | tf_op jit(solution)/shard_map/all_to_all | solution.py:446
  41.6 4.2 %collective-permute-start.1 = (bf16[8,16,640]{2,1,0:T(8,128)(2,1)S(1)}, bf16[8,16,640]{2,1,0:T(8,128)(2,1)S(1)}, u32[]{:S(2)}, u32[]{:S(2)}) collective-permute-start(bf16[8,16,640]{2,1,0:T(8,128)(2,1)S(1)} %all_to_all.11.own_ref), channel_id=1, source_target_pairs={{0,8},{8,16},{16,24},{24,32},{32,40},{40,48},{48,56},{56,64},{64,7... | collective-permute-start | bytes 491528 | tf_op jit(solution)/shard_map/ppermute | solution.py:449
  45.8 2.2 %collective-permute-done.1 = bf16[8,16,640]{2,1,0:T(8,128)(2,1)S(1)} collective-permute-done((bf16[8,16,640]{2,1,0:T(8,128)(2,1)S(1)}, bf16[8,16,640]{2,1,0:T(8,128)(2,1)S(1)}, u32[]{:S(2)}, u32[]{:S(2)}) %collective-permute-start.1) | collective-permute-done | bytes 163872 | tf_op jit(solution)/shard_map/ppermute | solution.py:449
  48.0 6.0 %all-gather.1 = bf16[16,16,640]{2,1,0:T(8,128)(2,1)S(1)} all-gather(bf16[8,16,640]{2,1,0:T(8,128)(2,1)S(1)} %collective-permute-done.1), channel_id=3, replica_groups=mesh['chip'=64,'core'=2,'tgt'=4] {'core'}, dimensions={0}, use_global_device_ids=true | all-gather | bytes 491520 | tf_op jit(solution)/shard_map/all_gather | solution.py:458
  54.0 5.8 %stokes.1 = (f32[3,4,578]{2,1,0:T(4,128)}, f32[3,4,578]{2,1,0:T(4,128)}) custom-call(bf16[8,16,640]{2,1,0:T(8,128)(2,1)S(1)} %all_to_all.11.own_ref, bf16[2,8,16,640]{3,2,1,0:T(8,128)(2,1)S(1)} %bitcast.13, f32[8,8,304]{2,1,0:T(8,128)S(1)} %get-tuple-element.22.targets, f32[8,8,128]{2,1,0:T(8,128)S(1)} %get-tuple-element.23.means, ...), custom_call_target="tpu_custom_call" | custom-call | tf_op jit(solution)/shard_map/stokes/pallas_call | solution.py:570
Async XLA Ops:
  11.9 8.7 %collective-permute-start = (bf16[8,16,640]{2,1,0:T(8,128)(2,1)S(1)}, bf16[8,16,640]{2,1,0:T(8,128)(2,1)S(1)}, u32[]{:S(2)}, u32[]{:S(2)}) collective-permute-start(bf16[8,16,640]{2,1,0:T(8,128)(2,1)S(1)} %all_to_all.10.own_ref), channel_id=1, source_target_pairs={{0,8},{8,16},{16,24},{24,32},{32,40},{40,48},{48,56},{56,64},{64,7... | collective-permute-start | bytes 491528 | tf_op jit(solution)/shard_map/ppermute | solution.py:449
  41.6 6.4 %collective-permute-start.1 = (bf16[8,16,640]{2,1,0:T(8,128)(2,1)S(1)}, bf16[8,16,640]{2,1,0:T(8,128)(2,1)S(1)}, u32[]{:S(2)}, u32[]{:S(2)}) collective-permute-start(bf16[8,16,640]{2,1,0:T(8,128)(2,1)S(1)} %all_to_all.11.own_ref), channel_id=1, source_target_pairs={{0,8},{8,16},{16,24},{24,32},{32,40},{40,48},{48,56},{56,64},{64,7... | collective-permute-start | bytes 491528 | tf_op jit(solution)/shard_map/ppermute | solution.py:449

commit v4 on v3

--- a/solution.py
+++ b/solution.py
@@ -13,7 +13,7 @@
 VMEM = pl.BlockSpec(memory_space=pltpu.VMEM)
 HBM = pl.BlockSpec(memory_space=pltpu.HBM)
 SMEM = pl.BlockSpec(memory_space=pltpu.SMEM)
-VECTOR_CHUNKS = (2, 5, 8)
+VECTOR_CHUNKS = (7, 8)
 LIMIT = (2 << 20, 20 << 20, 20 << 20)
 
 
@@ -284,7 +284,7 @@
 
     def work(k, src, coefs, qrow):
         tgt = feats[k]
-        total = jnp.zeros((wide, 16), jnp.float32)
+        cubes = []
         for lo in range(0, fine_nodes, 256):
             hi = min(lo + 256, fine_nodes)
             if lo // 256 in VECTOR_CHUNKS:
@@ -300,12 +300,13 @@
                 dist = jnp.dot(tgt, src[:, lo:hi], preferred_element_type=jnp.float32)
                 cube = inverse_cube(dist)
             cube_ref[k, :, lo:hi] = cube
-            total = total + lax.dot_general(
-                cube,
-                coefs[:, lo:hi],
-                (((1,), (1,)), ((), ())),
-                preferred_element_type=jnp.float32,
-            )
+            cubes.append(cube)
+        total = lax.dot_general(
+            jnp.concatenate(cubes, axis=1),
+            coefs[...],
+            (((1,), (1,)), ((), ())),
+            preferred_element_type=jnp.float32,
+        )
         sums = total.T
         sums = sums[0:8] + sums[8:16]
         sums = sums + jnp.concatenate([sums[4:8], sums[0:4]], axis=0)

time: 60.1 us -> 59.4 us (0.988)
  Pallas kernels: 17.1 us -> 16.4 us
    pallas_call x1, Pallas kernels: 8.46 us -> 7.73 us  [local(): pl.pallas_call(functools.partial(field_kernel, nodes), out_shape=(shape((...]
where the time goes in v4:
time: 59.4 us; the launch traced here: 59.1 us
  blocking collectives  28.9 us (49%)
  Pallas kernels  16.4 us (28%)
  starting transfers between devices  10.2 us (17%)
  waiting for transfers between devices  2.24 us (4%)
  between operations  1.33 us (2%)
    all_to_all x2, blocking collectives, exchange(): own = lax.all_to_all(mine, ('core', 'tgt'), 0, 0)  19.2 us
    ppermute x2, starting transfers between devices, exchange(): side = lax.ppermute(own, ('chip', 'core'), moves)  10.2 us
    all_gather x2, blocking collectives, share(): return lax.all_gather(side, 'core')  9.68 us
    pallas_call x1, Pallas kernels, local(): pl.pallas_call(functools.partial(field_kernel, nodes), out_shape=(shape((...  7.73 us
    pallas_call x1, Pallas kernels, local(): pl.pallas_call(functools.partial(stokes_kernel, nodes), out_shape=(shape(...  5.75 us
    ppermute x2, waiting for transfers between devices, exchange(): side = lax.ppermute(own, ('chip', 'core'), moves)  2.24 us
    pallas_call x1, Pallas kernels, local(): pl.pallas_call(target_kernel, out_shape=(shape((pairs, wide, 32), bf16),...  2.05 us
  transfers between devices with their start and end apart: 2, of which 1 were waited for; matrix products, arithmetic and copies ran while one was open for 0% of the time, Pallas kernels for 3%

profile of v4, /device:TPU:385, one launch (start us, length us, event | category | flops | bytes accessed | tf_op | source)
XLA Modules:
  0.0 59.1 jit_solution(7278679726738005850)
XLA Ops:
  0.6 0.8 %pack.1 = bf16[8,16,640]{2,1,0:T(8,128)(2,1)S(1)} custom-call(s32[4,5]{1,0:T(4,128)} %bitcast.17, f32[3,4,578]{2,1,0:T(4,128)} %bitcast.14, f32[4,578]{1,0:T(4,128)} %charge_hbm.1, f32[4,578]{1,0:T(4,128)} %weight_hbm.3), custom_call_target="tpu_custom_call" | custom-call | tf_op jit(solution)/shard_map/pack/pallas_call | solution.py:490
  1.5 10.4 %all_to_all.10.own_ref = bf16[8,16,640]{2,1,0:T(8,128)(2,1)S(1)} all-to-all(bf16[8,16,640]{2,1,0:T(8,128)(2,1)S(1)} %pack.1), channel_id=1, replica_groups=mesh['chip'=64,'core'=2,'tgt'=4] {'core','tgt'}, dimensions={0} | all-to-all | bytes 327680 | tf_op jit(solution)/shard_map/all_to_all | solution.py:447
  11.9 6.0 %collective-permute-start = (bf16[8,16,640]{2,1,0:T(8,128)(2,1)S(1)}, bf16[8,16,640]{2,1,0:T(8,128)(2,1)S(1)}, u32[]{:S(2)}, u32[]{:S(2)}) collective-permute-start(bf16[8,16,640]{2,1,0:T(8,128)(2,1)S(1)} %all_to_all.10.own_ref), channel_id=1, source_target_pairs={{0,8},{8,16},{16,24},{24,32},{32,40},{40,48},{48,56},{56,64},{64,7... | collective-permute-start | bytes 491528 | tf_op jit(solution)/shard_map/ppermute | solution.py:450
  18.6 2.0 %target.1 = (bf16[8,304,32]{2,1,0:T(8,128)(2,1)S(1)}, f32[8,8,304]{2,1,0:T(8,128)S(1)}, f32[8,8,128]{2,1,0:T(8,128)S(1)}, f32[8,4,304,128]{3,2,1,0:T(8,128)S(1)}...) custom-call(s32[1,1]{1,0:T(1,128)S(6)} %copy.12.count_ref, ...), custom_call_target="tpu_custom_call" | custom-call | flops 4000000 | bytes 6000000 | tf_op jit(solution)/shard_map/target/pallas_call | solution.py:509
  20.6 0.0 collective-permute-done
  20.6 3.7 %all-gather = bf16[16,16,640]{2,1,0:T(8,128)(2,1)S(1)} all-gather(bf16[8,16,640]{2,1,0:T(8,128)(2,1)S(1)} %collective-permute-done), channel_id=2, replica_groups=mesh['chip'=64,'core'=2,'tgt'=4] {'core'}, dimensions={0}, use_global_device_ids=true | all-gather | bytes 491520 | tf_op jit(solution)/shard_map/all_gather | solution.py:459
  24.3 7.7 %field.1 = (f32[3,4,578]{2,1,0:T(4,128)S(1)}, bf16[8,16,640]{2,1,0:T(8,128)(2,1)S(1)}, bf16[8,304,2112]{2,1,0:T(8,128)(2,1)S(1)}, bf16[64,384]{1,0:T(8,128)(2,1)S(1)}, f32[8,8,2112]{2,1,0:T(8,128)S(1)}) custom-call(bf16[8,16,640]{2,1,0:T(8,128)(2,1)S(1)} %all_to_all.10.own_ref, bf16[2,8,16,640]{3,2,1,0:T(8,128)(2,1)S(1)} %bitcast.12, ...), custom_call_target="tpu_custom_call" | custom-call | tf_op jit(solution)/shard_map/field/pallas_call | solution.py:544
  32.1 8.8 %all_to_all.11.own_ref = bf16[8,16,640]{2,1,0:T(8,128)(2,1)S(1)} all-to-all(bf16[8,16,640]{2,1,0:T(8,128)(2,1)S(1)} %get-tuple-element.33), channel_id=1, replica_groups=mesh['chip'=64,'core'=2,'tgt'=4] {'core','tgt'}, dimensions={0} | all-to-all | bytes 327680 | tf_op jit(solution)/shard_map/all_to_all | solution.py:447
  40.9 4.2 %collective-permute-start.1 = (bf16[8,16,640]{2,1,0:T(8,128)(2,1)S(1)}, bf16[8,16,640]{2,1,0:T(8,128)(2,1)S(1)}, u32[]{:S(2)}, u32[]{:S(2)}) collective-permute-start(bf16[8,16,640]{2,1,0:T(8,128)(2,1)S(1)} %all_to_all.11.own_ref), channel_id=1, source_target_pairs={{0,8},{8,16},{16,24},{24,32},{32,40},{40,48},{48,56},{56,64},{64,7... | collective-permute-start | bytes 491528 | tf_op jit(solution)/shard_map/ppermute | solution.py:450
  45.1 2.2 %collective-permute-done.1 = bf16[8,16,640]{2,1,0:T(8,128)(2,1)S(1)} collective-permute-done((bf16[8,16,640]{2,1,0:T(8,128)(2,1)S(1)}, bf16[8,16,640]{2,1,0:T(8,128)(2,1)S(1)}, u32[]{:S(2)}, u32[]{:S(2)}) %collective-permute-start.1) | collective-permute-done | bytes 163872 | tf_op jit(solution)/shard_map/ppermute | solution.py:450
  47.3 6.0 %all-gather.1 = bf16[16,16,640]{2,1,0:T(8,128)(2,1)S(1)} all-gather(bf16[8,16,640]{2,1,0:T(8,128)(2,1)S(1)} %collective-permute-done.1), channel_id=3, replica_groups=mesh['chip'=64,'core'=2,'tgt'=4] {'core'}, dimensions={0}, use_global_device_ids=true | all-gather | bytes 491520 | tf_op jit(solution)/shard_map/all_gather | solution.py:459
  53.3 5.8 %stokes.1 = (f32[3,4,578]{2,1,0:T(4,128)}, f32[3,4,578]{2,1,0:T(4,128)}) custom-call(bf16[8,16,640]{2,1,0:T(8,128)(2,1)S(1)} %all_to_all.11.own_ref, bf16[2,8,16,640]{3,2,1,0:T(8,128)(2,1)S(1)} %bitcast.13, f32[8,8,304]{2,1,0:T(8,128)S(1)} %get-tuple-element.22.targets, f32[8,8,128]{2,1,0:T(8,128)S(1)} %get-tuple-element.23.means, ...), custom_call_target="tpu_custom_call" | custom-call | tf_op jit(solution)/shard_map/stokes/pallas_call | solution.py:571
Async XLA Ops:
  11.9 8.7 %collective-permute-start = (bf16[8,16,640]{2,1,0:T(8,128)(2,1)S(1)}, bf16[8,16,640]{2,1,0:T(8,128)(2,1)S(1)}, u32[]{:S(2)}, u32[]{:S(2)}) collective-permute-start(bf16[8,16,640]{2,1,0:T(8,128)(2,1)S(1)} %all_to_all.10.own_ref), channel_id=1, source_target_pairs={{0,8},{8,16},{16,24},{24,32},{32,40},{40,48},{48,56},{56,64},{64,7... | collective-permute-start | bytes 491528 | tf_op jit(solution)/shard_map/ppermute | solution.py:450
  40.9 6.4 %collective-permute-start.1 = (bf16[8,16,640]{2,1,0:T(8,128)(2,1)S(1)}, bf16[8,16,640]{2,1,0:T(8,128)(2,1)S(1)}, u32[]{:S(2)}, u32[]{:S(2)}) collective-permute-start(bf16[8,16,640]{2,1,0:T(8,128)(2,1)S(1)} %all_to_all.11.own_ref), channel_id=1, source_target_pairs={{0,8},{8,16},{16,24},{24,32},{32,40},{40,48},{48,56},{56,64},{64,7... | collective-permute-start | bytes 491528 | tf_op jit(solution)/shard_map/ppermute | solution.py:450

commit v5 on v4

--- a/solution.py
+++ b/solution.py
@@ -138,8 +138,8 @@
     want = jnp.zeros((height, 128), jnp.int32)
     for k in range(pairs):
         p = slot_ref[0, k]
-        start = jnp.where(row // 8 == k, block_index(p, core), start)
-        want = jnp.where(row // 8 == k, nodes % 128 + p % 20, want)
+        start = jnp.where(row // 4 == k, block_index(p, core), start)
+        want = jnp.where(row // 4 == k, nodes % 128 + p % 20, want)
     lane = iota((height, 128), 1)
     base_ref[...] = start + (row % 4) * 4
     want_ref[...] = want
@@ -242,7 +242,7 @@
     wide = feats.shape[1]
     fine_nodes = up_ref.shape[1]
 
-    height = pairs * 8
+    height = pairs * 4
     lane_id = iota((height, 128), 1)
     table = select(head_ref[...], own_ref, side_ref, nodes // 128 * 128)
     chosen = jnp.sum(
@@ -259,7 +259,8 @@
         preferred_element_type=jnp.float32,
     )
     for k in range(pairs):
-        fine_ref[k] = fine[k * 8 : (k + 1) * 8]
+        one = fine[k * 4 : (k + 1) * 4]
+        fine_ref[k] = jnp.concatenate([one, one], axis=0)
 
     sub_f = iota((8, fine_nodes), 0)
 
@@ -377,7 +378,8 @@
         preferred_element_type=jnp.float32,
     )
     for k in range(pairs):
-        forces[k] = fine[k * 8 : (k + 1) * 8]
+        one = fine[k * 4 : (k + 1) * 4]
+        forces[k] = jnp.concatenate([one, one], axis=0)
 
     sub_f = iota((8, fine_nodes), 0)
 
@@ -426,15 +428,10 @@
 
     prepare(0, coef_a)
 
-    def two_pairs(i, carry):
-        k = 2 * i
-        prepare(k + 1, coef_b)
-        work(k, coef_a)
-        prepare(jnp.minimum(k + 2, pairs - 1), coef_a)
-        work(k + 1, coef_b)
-        return carry
-
-    lax.fori_loop(0, pairs // 2, two_pairs, 0)
+    for k in range(pairs):
+        if k + 1 < pairs:
+            prepare(k + 1, coef_a if k % 2 else coef_b)
+        work(k, coef_b if k % 2 else coef_a)
     for d in range(drops):
         for h, (lo, hi) in enumerate(tile_slices(nodes)):
             flow = gather_tiles(values, mask_ref, d * 2 + h, 3)
@@ -513,9 +510,9 @@
             shape((pairs, 8, wide), f32),
             shape((pairs, 8, 128), f32),
             shape((pairs, 4, wide, 128), f32),
-            shape((pairs * 8, 384), bf16),
-            shape((pairs * 8, 128), i32),
-            shape((pairs * 8, 128), i32),
+            shape((pairs * 4, 384), bf16),
+            shape((pairs * 4, 128), i32),
+            shape((pairs * 4, 128), i32),
             shape((tiles, pairs, wide), f32),
             shape((3, drops, lanes), f32),
             shape(upsample.shape, bf16),
@@ -547,7 +544,7 @@
             shape((3, drops, nodes), f32),
             shape((8, 16, lanes), bf16),
             shape((pairs, wide, fine_nodes), bf16),
-            shape((pairs * 8, 384), bf16),
+            shape((pairs * 4, 384), bf16),
             shape((pairs, 8, fine_nodes), f32),
         ),
         in_specs=[VMEM] * 14,

time: 59.4 us -> 58.1 us (0.978)
  the two profiles are of different devices: /device:TPU:385 before, /device:TPU:257 now
where the time goes in v5:
time: 58.1 us; the launch traced here: 57.8 us
  blocking collectives  31.4 us (54%)
  Pallas kernels  15.1 us (26%)
  starting transfers between devices  6.01 us (10%)
  waiting for transfers between devices  3.96 us (7%)
  between operations  1.33 us (2%)
    all_to_all x2, blocking collectives, exchange(): own = lax.all_to_all(mine, ('core', 'tgt'), 0, 0)  19.2 us
    all_gather x2, blocking collectives, share(): return lax.all_gather(side, 'core')  12.2 us
    pallas_call x1, Pallas kernels, local(): pl.pallas_call(functools.partial(field_kernel, nodes), out_shape=(shape((...  7.69 us
    ppermute x2, starting transfers between devices, exchange(): side = lax.ppermute(own, ('chip', 'core'), moves)  6.01 us
    pallas_call x1, Pallas kernels, local(): pl.pallas_call(functools.partial(stokes_kernel, nodes), out_shape=(shape(...  4.56 us
    ppermute x2, waiting for transfers between devices, exchange(): side = lax.ppermute(own, ('chip', 'core'), moves)  3.96 us
    pallas_call x1, Pallas kernels, local(): pl.pallas_call(target_kernel, out_shape=(shape((pairs, wide, 32), bf16),...  2.05 us
  transfers between devices with their start and end apart: 2, of which 1 were waited for; matrix products, arithmetic and copies ran while one was open for 0% of the time, Pallas kernels for 4%

profile of v5, /device:TPU:257, one launch (start us, length us, event | category | flops | bytes accessed | tf_op | source)
XLA Modules:
  0.0 57.8 jit_solution(17131538981453721690)
XLA Ops:
  0.6 0.8 %pack.1 = bf16[8,16,640]{2,1,0:T(8,128)(2,1)S(1)} custom-call(s32[4,5]{1,0:T(4,128)} %bitcast.17, f32[3,4,578]{2,1,0:T(4,128)} %bitcast.14, f32[4,578]{1,0:T(4,128)} %charge_hbm.1, f32[4,578]{1,0:T(4,128)} %weight_hbm.3), custom_call_target="tpu_custom_call" | custom-call | tf_op jit(solution)/shard_map/pack/pallas_call | solution.py:487
  1.5 10.4 %all_to_all.10.own_ref = bf16[8,16,640]{2,1,0:T(8,128)(2,1)S(1)} all-to-all(bf16[8,16,640]{2,1,0:T(8,128)(2,1)S(1)} %pack.1), channel_id=1, replica_groups=mesh['chip'=64,'core'=2,'tgt'=4] {'core','tgt'}, dimensions={0} | all-to-all | bytes 327680 | tf_op jit(solution)/shard_map/all_to_all | solution.py:444
  11.9 3.9 %collective-permute-start = (bf16[8,16,640]{2,1,0:T(8,128)(2,1)S(1)}, bf16[8,16,640]{2,1,0:T(8,128)(2,1)S(1)}, u32[]{:S(2)}, u32[]{:S(2)}) collective-permute-start(bf16[8,16,640]{2,1,0:T(8,128)(2,1)S(1)} %all_to_all.10.own_ref), channel_id=1, source_target_pairs={{0,8},{8,16},{16,24},{24,32},{32,40},{40,48},{48,56},{56,64},{64,7... | collective-permute-start | bytes 491528 | tf_op jit(solution)/shard_map/ppermute | solution.py:447
  16.5 2.1 %target.1 = (bf16[8,304,32]{2,1,0:T(8,128)(2,1)S(1)}, f32[8,8,304]{2,1,0:T(8,128)S(1)}, f32[8,8,128]{2,1,0:T(8,128)S(1)}, f32[8,4,304,128]{3,2,1,0:T(8,128)S(1)}...) custom-call(s32[1,1]{1,0:T(1,128)S(6)} %copy.12.count_ref, ...), custom_call_target="tpu_custom_call" | custom-call | flops 4000000 | bytes 6000000 | tf_op jit(solution)/shard_map/target/pallas_call | solution.py:506
  18.5 0.0 collective-permute-done
  18.5 5.8 %all-gather = bf16[16,16,640]{2,1,0:T(8,128)(2,1)S(1)} all-gather(bf16[8,16,640]{2,1,0:T(8,128)(2,1)S(1)} %collective-permute-done), channel_id=2, replica_groups=mesh['chip'=64,'core'=2,'tgt'=4] {'core'}, dimensions={0}, use_global_device_ids=true | all-gather | bytes 491520 | tf_op jit(solution)/shard_map/all_gather | solution.py:456
  24.3 7.7 %field.1 = (f32[3,4,578]{2,1,0:T(4,128)S(1)}, bf16[8,16,640]{2,1,0:T(8,128)(2,1)S(1)}, bf16[8,304,2112]{2,1,0:T(8,128)(2,1)S(1)}, bf16[32,384]{1,0:T(8,128)(2,1)S(1)}, f32[8,8,2112]{2,1,0:T(8,128)S(1)}) custom-call(bf16[8,16,640]{2,1,0:T(8,128)(2,1)S(1)} %all_to_all.10.own_ref, bf16[2,8,16,640]{3,2,1,0:T(8,128)(2,1)S(1)} %bitcast.12, ...), custom_call_target="tpu_custom_call" | custom-call | tf_op jit(solution)/shard_map/field/pallas_call | solution.py:541
  32.0 8.8 %all_to_all.11.own_ref = bf16[8,16,640]{2,1,0:T(8,128)(2,1)S(1)} all-to-all(bf16[8,16,640]{2,1,0:T(8,128)(2,1)S(1)} %get-tuple-element.33), channel_id=1, replica_groups=mesh['chip'=64,'core'=2,'tgt'=4] {'core','tgt'}, dimensions={0} | all-to-all | bytes 327680 | tf_op jit(solution)/shard_map/all_to_all | solution.py:444
  40.8 2.1 %collective-permute-start.1 = (bf16[8,16,640]{2,1,0:T(8,128)(2,1)S(1)}, bf16[8,16,640]{2,1,0:T(8,128)(2,1)S(1)}, u32[]{:S(2)}, u32[]{:S(2)}) collective-permute-start(bf16[8,16,640]{2,1,0:T(8,128)(2,1)S(1)} %all_to_all.11.own_ref), channel_id=1, source_target_pairs={{0,8},{8,16},{16,24},{24,32},{32,40},{40,48},{48,56},{56,64},{64,7... | collective-permute-start | bytes 491528 | tf_op jit(solution)/shard_map/ppermute | solution.py:447
  42.9 4.0 %collective-permute-done.1 = bf16[8,16,640]{2,1,0:T(8,128)(2,1)S(1)} collective-permute-done((bf16[8,16,640]{2,1,0:T(8,128)(2,1)S(1)}, bf16[8,16,640]{2,1,0:T(8,128)(2,1)S(1)}, u32[]{:S(2)}, u32[]{:S(2)}) %collective-permute-start.1) | collective-permute-done | bytes 163872 | tf_op jit(solution)/shard_map/ppermute | solution.py:447
  46.9 6.4 %all-gather.1 = bf16[16,16,640]{2,1,0:T(8,128)(2,1)S(1)} all-gather(bf16[8,16,640]{2,1,0:T(8,128)(2,1)S(1)} %collective-permute-done.1), channel_id=3, replica_groups=mesh['chip'=64,'core'=2,'tgt'=4] {'core'}, dimensions={0}, use_global_device_ids=true | all-gather | bytes 491520 | tf_op jit(solution)/shard_map/all_gather | solution.py:456
  53.3 4.6 %stokes.1 = (f32[3,4,578]{2,1,0:T(4,128)}, f32[3,4,578]{2,1,0:T(4,128)}) custom-call(bf16[8,16,640]{2,1,0:T(8,128)(2,1)S(1)} %all_to_all.11.own_ref, bf16[2,8,16,640]{3,2,1,0:T(8,128)(2,1)S(1)} %bitcast.13, f32[8,8,304]{2,1,0:T(8,128)S(1)} %get-tuple-element.22.targets, f32[8,8,128]{2,1,0:T(8,128)S(1)} %get-tuple-element.23.means, ...), custom_call_target="tpu_custom_call" | custom-call | tf_op jit(solution)/shard_map/stokes/pallas_call | solution.py:568
Async XLA Ops:
  11.9 6.6 %collective-permute-start = (bf16[8,16,640]{2,1,0:T(8,128)(2,1)S(1)}, bf16[8,16,640]{2,1,0:T(8,128)(2,1)S(1)}, u32[]{:S(2)}, u32[]{:S(2)}) collective-permute-start(bf16[8,16,640]{2,1,0:T(8,128)(2,1)S(1)} %all_to_all.10.own_ref), channel_id=1, source_target_pairs={{0,8},{8,16},{16,24},{24,32},{32,40},{40,48},{48,56},{56,64},{64,7... | collective-permute-start | bytes 491528 | tf_op jit(solution)/shard_map/ppermute | solution.py:447
  40.8 6.1 %collective-permute-start.1 = (bf16[8,16,640]{2,1,0:T(8,128)(2,1)S(1)}, bf16[8,16,640]{2,1,0:T(8,128)(2,1)S(1)}, u32[]{:S(2)}, u32[]{:S(2)}) collective-permute-start(bf16[8,16,640]{2,1,0:T(8,128)(2,1)S(1)} %all_to_all.11.own_ref), channel_id=1, source_target_pairs={{0,8},{8,16},{16,24},{24,32},{32,40},{40,48},{48,56},{56,64},{64,7... | collective-permute-start | bytes 491528 | tf_op jit(solution)/shard_map/ppermute | solution.py:447

commit v6 on v5

--- a/solution.py
+++ b/solution.py
@@ -315,15 +315,10 @@
 
     prepare(0, src_a, coef_a, row_a)
 
-    def two(i, carry):
-        k = 2 * i
-        prepare(k + 1, src_b, coef_b, row_b)
-        work(k, src_a, coef_a, row_a)
-        prepare(jnp.minimum(k + 2, pairs - 1), src_a, coef_a, row_a)
-        work(k + 1, src_b, coef_b, row_b)
-        return carry
-
-    lax.fori_loop(0, pairs // 2, two, 0)
+    for k in range(pairs):
+        if k + 1 < pairs:
+            prepare(k + 1, *((src_a, coef_a, row_a) if k % 2 else (src_b, coef_b, row_b)))
+        work(k, *((src_b, coef_b, row_b) if k % 2 else (src_a, coef_a, row_a)))
 
     block[...] = jnp.zeros_like(block)
     for d in range(drops):

time: 58.1 us -> 57 us (0.981)
  the two profiles are of different devices: /device:TPU:257 before, /device:TPU:385 now
where the time goes in v6:
time: 57 us; the launch traced here: 56.7 us
  blocking collectives  28.9 us (51%)
  Pallas kernels  14 us (25%)
  starting transfers between devices  10.2 us (18%)
  waiting for transfers between devices  2.24 us (4%)
  between operations  1.33 us (2%)
    all_to_all x2, blocking collectives, exchange(): own = lax.all_to_all(mine, ('core', 'tgt'), 0, 0)  19.2 us
    ppermute x2, starting transfers between devices, exchange(): side = lax.ppermute(own, ('chip', 'core'), moves)  10.2 us
    all_gather x2, blocking collectives, share(): return lax.all_gather(side, 'core')  9.69 us
    pallas_call x1, Pallas kernels, local(): pl.pallas_call(functools.partial(field_kernel, nodes), out_shape=(shape((...  6.58 us
    pallas_call x1, Pallas kernels, local(): pl.pallas_call(functools.partial(stokes_kernel, nodes), out_shape=(shape(...  4.56 us
    ppermute x2, waiting for transfers between devices, exchange(): side = lax.ppermute(own, ('chip', 'core'), moves)  2.24 us
    pallas_call x1, Pallas kernels, local(): pl.pallas_call(target_kernel, out_shape=(shape((pairs, wide, 32), bf16),...  2.03 us
  transfers between devices with their start and end apart: 2, of which 1 were waited for; matrix products, arithmetic and copies ran while one was open for 0% of the time, Pallas kernels for 4%

profile of v6, /device:TPU:385, one launch (start us, length us, event | category | flops | bytes accessed | tf_op | source)
XLA Modules:
  0.0 56.7 jit_solution(9801198318911567061)
XLA Ops:
  0.6 0.8 %pack.1 = bf16[8,16,640]{2,1,0:T(8,128)(2,1)S(1)} custom-call(s32[4,5]{1,0:T(4,128)} %bitcast.17, f32[3,4,578]{2,1,0:T(4,128)} %bitcast.14, f32[4,578]{1,0:T(4,128)} %charge_hbm.1, f32[4,578]{1,0:T(4,128)} %weight_hbm.3), custom_call_target="tpu_custom_call" | custom-call | tf_op jit(solution)/shard_map/pack/pallas_call | solution.py:482
  1.5 10.4 %all_to_all.10.own_ref = bf16[8,16,640]{2,1,0:T(8,128)(2,1)S(1)} all-to-all(bf16[8,16,640]{2,1,0:T(8,128)(2,1)S(1)} %pack.1), channel_id=1, replica_groups=mesh['chip'=64,'core'=2,'tgt'=4] {'core','tgt'}, dimensions={0} | all-to-all | bytes 327680 | tf_op jit(solution)/shard_map/all_to_all | solution.py:439
  11.9 6.0 %collective-permute-start = (bf16[8,16,640]{2,1,0:T(8,128)(2,1)S(1)}, bf16[8,16,640]{2,1,0:T(8,128)(2,1)S(1)}, u32[]{:S(2)}, u32[]{:S(2)}) collective-permute-start(bf16[8,16,640]{2,1,0:T(8,128)(2,1)S(1)} %all_to_all.10.own_ref), channel_id=1, source_target_pairs={{0,8},{8,16},{16,24},{24,32},{32,40},{40,48},{48,56},{56,64},{64,7... | collective-permute-start | bytes 491528 | tf_op jit(solution)/shard_map/ppermute | solution.py:442
  18.6 2.0 %target.1 = (bf16[8,304,32]{2,1,0:T(8,128)(2,1)S(1)}, f32[8,8,304]{2,1,0:T(8,128)S(1)}, f32[8,8,128]{2,1,0:T(8,128)S(1)}, f32[8,4,304,128]{3,2,1,0:T(8,128)S(1)}...) custom-call(s32[1,1]{1,0:T(1,128)S(6)} %copy.12.count_ref, ...), custom_call_target="tpu_custom_call" | custom-call | flops 4000000 | bytes 6000000 | tf_op jit(solution)/shard_map/target/pallas_call | solution.py:501
  20.6 0.0 collective-permute-done
  20.6 3.7 %all-gather = bf16[16,16,640]{2,1,0:T(8,128)(2,1)S(1)} all-gather(bf16[8,16,640]{2,1,0:T(8,128)(2,1)S(1)} %collective-permute-done), channel_id=2, replica_groups=mesh['chip'=64,'core'=2,'tgt'=4] {'core'}, dimensions={0}, use_global_device_ids=true | all-gather | bytes 491520 | tf_op jit(solution)/shard_map/all_gather | solution.py:451
  24.3 6.6 %field.1 = (f32[3,4,578]{2,1,0:T(4,128)S(1)}, bf16[8,16,640]{2,1,0:T(8,128)(2,1)S(1)}, bf16[8,304,2112]{2,1,0:T(8,128)(2,1)S(1)}, bf16[32,384]{1,0:T(8,128)(2,1)S(1)}, f32[8,8,2112]{2,1,0:T(8,128)S(1)}) custom-call(bf16[8,16,640]{2,1,0:T(8,128)(2,1)S(1)} %all_to_all.10.own_ref, bf16[2,8,16,640]{3,2,1,0:T(8,128)(2,1)S(1)} %bitcast.12, ...), custom_call_target="tpu_custom_call" | custom-call | tf_op jit(solution)/shard_map/field/pallas_call | solution.py:536
  30.9 8.8 %all_to_all.11.own_ref = bf16[8,16,640]{2,1,0:T(8,128)(2,1)S(1)} all-to-all(bf16[8,16,640]{2,1,0:T(8,128)(2,1)S(1)} %get-tuple-element.33), channel_id=1, replica_groups=mesh['chip'=64,'core'=2,'tgt'=4] {'core','tgt'}, dimensions={0} | all-to-all | bytes 327680 | tf_op jit(solution)/shard_map/all_to_all | solution.py:439
  39.7 4.2 %collective-permute-start.1 = (bf16[8,16,640]{2,1,0:T(8,128)(2,1)S(1)}, bf16[8,16,640]{2,1,0:T(8,128)(2,1)S(1)}, u32[]{:S(2)}, u32[]{:S(2)}) collective-permute-start(bf16[8,16,640]{2,1,0:T(8,128)(2,1)S(1)} %all_to_all.11.own_ref), channel_id=1, source_target_pairs={{0,8},{8,16},{16,24},{24,32},{32,40},{40,48},{48,56},{56,64},{64,7... | collective-permute-start | bytes 491528 | tf_op jit(solution)/shard_map/ppermute | solution.py:442
  43.9 2.2 %collective-permute-done.1 = bf16[8,16,640]{2,1,0:T(8,128)(2,1)S(1)} collective-permute-done((bf16[8,16,640]{2,1,0:T(8,128)(2,1)S(1)}, bf16[8,16,640]{2,1,0:T(8,128)(2,1)S(1)}, u32[]{:S(2)}, u32[]{:S(2)}) %collective-permute-start.1) | collective-permute-done | bytes 163872 | tf_op jit(solution)/shard_map/ppermute | solution.py:442
  46.2 6.0 %all-gather.1 = bf16[16,16,640]{2,1,0:T(8,128)(2,1)S(1)} all-gather(bf16[8,16,640]{2,1,0:T(8,128)(2,1)S(1)} %collective-permute-done.1), channel_id=3, replica_groups=mesh['chip'=64,'core'=2,'tgt'=4] {'core'}, dimensions={0}, use_global_device_ids=true | all-gather | bytes 491520 | tf_op jit(solution)/shard_map/all_gather | solution.py:451
  52.1 4.6 %stokes.1 = (f32[3,4,578]{2,1,0:T(4,128)}, f32[3,4,578]{2,1,0:T(4,128)}) custom-call(bf16[8,16,640]{2,1,0:T(8,128)(2,1)S(1)} %all_to_all.11.own_ref, bf16[2,8,16,640]{3,2,1,0:T(8,128)(2,1)S(1)} %bitcast.13, f32[8,8,304]{2,1,0:T(8,128)S(1)} %get-tuple-element.22.targets, f32[8,8,128]{2,1,0:T(8,128)S(1)} %get-tuple-element.23.means, ...), custom_call_target="tpu_custom_call" | custom-call | tf_op jit(solution)/shard_map/stokes/pallas_call | solution.py:563
Async XLA Ops:
  11.9 8.7 %collective-permute-start = (bf16[8,16,640]{2,1,0:T(8,128)(2,1)S(1)}, bf16[8,16,640]{2,1,0:T(8,128)(2,1)S(1)}, u32[]{:S(2)}, u32[]{:S(2)}) collective-permute-start(bf16[8,16,640]{2,1,0:T(8,128)(2,1)S(1)} %all_to_all.10.own_ref), channel_id=1, source_target_pairs={{0,8},{8,16},{16,24},{24,32},{32,40},{40,48},{48,56},{56,64},{64,7... | collective-permute-start | bytes 491528 | tf_op jit(solution)/shard_map/ppermute | solution.py:442
  39.7 6.4 %collective-permute-start.1 = (bf16[8,16,640]{2,1,0:T(8,128)(2,1)S(1)}, bf16[8,16,640]{2,1,0:T(8,128)(2,1)S(1)}, u32[]{:S(2)}, u32[]{:S(2)}) collective-permute-start(bf16[8,16,640]{2,1,0:T(8,128)(2,1)S(1)} %all_to_all.11.own_ref), channel_id=1, source_target_pairs={{0,8},{8,16},{16,24},{24,32},{32,40},{40,48},{48,56},{56,64},{64,7... | collective-permute-start | bytes 491528 | tf_op jit(solution)/shard_map/ppermute | solution.py:442
